TPU v7x, 128 devices: a whole 4x4x4 slice. The times are simulated.
128 devices in a mesh: pb: 16 (over z_hi, y, core), ka: 8 (over z_lo, x).
Axes of the slice: x: 4, y: 4, z: 4 (z_hi: 2, z_lo: 2; z = z_hi * 2 + z_lo), core: 2. Of those that a mesh axis runs over, the one named last changes fastest.
Arguments:
- query_features: bfloat16 [128, 192, 256], P('pb'), may hold values from -6 to 6
- key_features: bfloat16 [192, 128, 256], P(None, 'ka'), may hold values from -6 to 6
- pyramid_grad: bfloat16 [24576, 8, 4080], P('pb', 'ka'), may hold values from -13.0639453 to 13.0639453
- query_image: bfloat16 [128, 192, 256], P('pb', 'ka'), may hold values from -0.0625 to 0.0625
- key_image: bfloat16 [192, 128, 256], P('pb', 'ka'), may hold values from -0.0625 to 0.0625
- conv_weight: bfloat16 [3, 3, 256, 256], replicated, may hold values from -0.125 to 0.125
Outputs:
- query_image_grad: bfloat16 [128, 192, 256], P('pb', 'ka')
- key_image_grad: bfloat16 [192, 128, 256], P('pb', 'ka')
- weight_grad: float32 [3, 3, 256, 256], replicated
All inputs are finite; a program needn't handle non-finite values.
Results may differ from a plain program's by a relative error of at most 0.0056.
Values may be sent and summed in bfloat16 or wider, within the bound.
A program may use at most 128 MiB of HBM per device.

v0:
```python
import jax
import jax.numpy as jnp
from jax import lax
from jax.sharding import PartitionSpec as P

D = 256
LEVELS = 4


def padded(cells, sides, width):
    for axis, dim in sides:
        count = lax.axis_size(axis)
        ends = count - 1
        head = lax.slice_in_dim(cells, 0, width, axis=dim)
        tail = lax.slice_in_dim(cells, cells.shape[dim] - width, cells.shape[dim], axis=dim)
        cells = jnp.concatenate(
            [
                lax.ppermute(tail, axis, [(i, (i + 1) % count) for i in range(ends)]),
                cells,
                lax.ppermute(head, axis, [((i + 1) % count, i) for i in range(ends)]),
            ],
            axis=dim,
        )
    return cells


def pool_levels(strip):
    strip_float = strip.astype(jnp.float32)
    result = []
    for level_index in range(LEVELS):
        factor = 2**level_index
        cell_cols, key_rows, channels = strip_float.shape
        pooled = strip_float.reshape(
            cell_cols // factor, factor, key_rows // factor, factor, channels
        ).mean(axis=(1, 3))
        result.append(pooled.astype(jnp.bfloat16))
    return result


def conv_backward(padded_input, padded_grad, kernel):
    tile_rows = padded_grad.shape[0] - 2
    tile_cols = padded_grad.shape[1] - 2
    out_channels = padded_grad.shape[2]
    in_channels = kernel.shape[2]
    interior = padded_grad[1 : 1 + tile_rows, 1 : 1 + tile_cols].reshape(-1, out_channels)
    input_acc = jnp.zeros((tile_rows * tile_cols, in_channels), jnp.float32)
    kernel_rows = []
    for row_shift in range(3):
        kernel_row = []
        for col_shift in range(3):
            shifted = padded_grad[
                2 - row_shift : 2 - row_shift + tile_rows, 2 - col_shift : 2 - col_shift + tile_cols
            ].reshape(-1, out_channels)
            input_acc = input_acc + lax.dot_general(
                shifted,
                kernel[row_shift, col_shift],
                (((1,), (1,)), ((), ())),
                preferred_element_type=jnp.float32,
            )
            window = padded_input[
                row_shift : row_shift + tile_rows, col_shift : col_shift + tile_cols
            ].reshape(-1, in_channels)
            weight_term = lax.dot_general(
                window, interior, (((0,), (0,)), ((), ())), preferred_element_type=jnp.float32
            )
            kernel_row.append(weight_term)
        kernel_rows.append(jnp.stack(kernel_row))
    return (input_acc.reshape(tile_rows, tile_cols, in_channels), jnp.stack(kernel_rows))


def body(query_features, key_features, pyramid_grad, query_image, key_image, conv_weight):
    norm_scale = D ** (-0.5)
    strip_rows, width_cells, channels = query_features.shape
    key_rows = key_features.shape[1]
    queries = query_features.reshape(strip_rows * width_cells, channels)
    strip_grads = pyramid_grad.reshape(pyramid_grad.shape[0], pyramid_grad.shape[2])
    pooled = pool_levels(key_features)
    query_part = jnp.zeros((queries.shape[0], channels), jnp.float32)
    coarse_sum = jnp.zeros((width_cells, key_rows, channels), jnp.float32)
    level_zero = None
    offset = 0
    for level_index in range(LEVELS):
        factor = 2**level_index
        grid_rows = key_rows // factor
        grid_cols = width_cells // factor
        cell_count = grid_rows * grid_cols
        grad_block = strip_grads[:, offset : offset + cell_count]
        offset = offset + cell_count
        ordered = jnp.transpose(pooled[level_index], (1, 0, 2)).reshape(cell_count, channels)
        query_part = query_part + jnp.dot(grad_block, ordered, preferred_element_type=jnp.float32)
        if level_index == 0:
            level_zero = grad_block.reshape(-1, grid_rows, grid_cols)
        else:
            coarse = lax.dot_general(
                grad_block, queries, (((0,), (0,)), ((), ())), preferred_element_type=jnp.float32
            )
            coarse = jnp.transpose(coarse.reshape(grid_rows, grid_cols, channels), (1, 0, 2))
            spread = jnp.broadcast_to(
                coarse[:, None, :, None, :], (grid_cols, factor, grid_rows, factor, channels)
            ).reshape(width_cells, key_rows, channels)
            coarse_sum = coarse_sum + spread / 4.0**level_index
    query_grad = lax.psum_scatter(
        (query_part * norm_scale).reshape(strip_rows, width_cells, channels),
        "ka",
        scatter_dimension=1,
        tiled=True,
    ).astype(jnp.bfloat16)
    fine_term = jnp.einsum("qhw,qd->whd", level_zero, queries, preferred_element_type=jnp.float32)
    key_grad = lax.psum_scatter(
        (fine_term + coarse_sum) * norm_scale, "pb", scatter_dimension=0, tiled=True
    ).astype(jnp.bfloat16)
    padded_query_image, padded_query_grad, padded_key_image, padded_key_grad = (
        padded(query_image, (("pb", 0), ("ka", 1)), 1),
        padded(query_grad, (("pb", 0), ("ka", 1)), 1),
        padded(key_image, (("pb", 0), ("ka", 1)), 1),
        padded(key_grad, (("pb", 0), ("ka", 1)), 1),
    )
    kernel_swapped = jnp.transpose(conv_weight, (1, 0, 2, 3))
    grad_first, weight_first = conv_backward(padded_query_image, padded_query_grad, conv_weight)
    grad_second, weight_swapped = conv_backward(padded_key_image, padded_key_grad, kernel_swapped)
    local_weight = weight_first + jnp.transpose(weight_swapped, (1, 0, 2, 3))
    weight_grad = lax.psum(local_weight, ("pb", "ka"))
    return (grad_first.astype(jnp.bfloat16), grad_second.astype(jnp.bfloat16), weight_grad)


def solution(mesh):
    placed = (
        P("pb", None, None),
        P(None, "ka", None),
        P("pb", "ka", None),
        P("pb", "ka", None),
        P("pb", "ka", None),
        P(),
    )
    return jax.shard_map(
        body,
        mesh=mesh,
        in_specs=placed,
        out_specs=(P("pb", "ka", None), P("pb", "ka", None), P()),
        check_vma=False,
    )
```

profile of v0, /device:TPU:1, one launch (start us, length us, event | category | flops | bytes accessed | tf_op | source)
XLA Modules:
  0.0 347.2 jit_solution(3468012486653483771)
XLA Ops:
  7.2 4.6 %reshape.140 = f32[96,2,8,2,256]{4,3,2,1,0:T(2,128)} reshape(bf16[192,16,256]{2,1,0:T(8,128)(2,1)} %param.7) | data formatting | bytes 4718592 | tf_op jit(solution)/shard_map/reshape | solution.py:33
  11.8 1.7 copy.47
  13.5 2.5 reshape.142
  16.0 2.2 convert_element_type.43
  18.2 4.4 %reduce_sum.27 = f32[96,8,256]{2,1,0:T(8,128)S(1)} reduce(f32[96,2,8,2,256]{4,3,2,1,0:T(2,128)} %reshape.140, f32[]{:T(128)} %constant.6.clone.1), dimensions={1,3}, to_apply=%region_0.0 | reduce | flops 589824 | bytes 3932164 | tf_op jit(solution)/shard_map/reduce_sum | solution.py:35
  22.7 3.0 reduce_sum.32
  25.8 2.4 reduce_sum.33
  28.2 2.8 convolution_bitcast_fusion.2
  31.1 5.2 %fusion.4 = f32[1536,256]{1,0:T(8,128)S(1)} fusion(f32[1536,256]{1,0:T(8,128)S(1)} %convolution_bitcast_fusion.2, bf16[3072,256]{1,0:T(8,128)(2,1)S(1)} %bitcast.277, bf16[1536,4080]{0,1:T(8,128)(2,1)} %bitcast.279), kind=kOutput, calls=%fused_computation.5 | convolution fusion | flops 2416312320 | bytes 14155776 | tf_op jit(solution)/shard_map/dot_general | solution.py:90
  36.3 1.5 fusion.9
  37.8 2.5 fusion.8
  41.2 4.6 %collective-permute-start.12 = (bf16[1,16,256]{2,1,0:T(8,128)(2,1)S(1)}, bf16[1,16,256]{2,1,0:T(8,128)(2,1)S(1)}, u32[]{:S(2)}, u32[]{:S(2)}) collective-permute-start(bf16[1,16,256]{2,1,0:T(8,128)(2,1)S(1)} %get-tuple-element.28), channel_id=1, source_target_pairs={{0,8},{8,16},{16,24},{24,32},{32,40},{40,48},{48,56},{56,64},{64,7... | collective-permute-start | bytes 24584 | tf_op jit(solution)/shard_map/ppermute | solution.py:18
  45.8 1.9 collective-permute-start.13
  47.7 3.6 %collective-permute-start.8 = (bf16[1,24,256]{2,1,0:T(8,128)(2,1)S(1)}, bf16[1,24,256]{2,1,0:T(8,128)(2,1)S(1)}, u32[]{:S(2)}, u32[]{:S(2)}) collective-permute-start(bf16[1,24,256]{2,1,0:T(8,128)(2,1)S(1)} %get-tuple-element.30), channel_id=1, source_target_pairs={{0,8},{8,16},{16,24},{24,32},{32,40},{40,48},{48,56},{56,64},{64,7... | collective-permute-start | bytes 36872 | tf_op jit(solution)/shard_map/ppermute | solution.py:18
  51.4 2.1 collective-permute-start.9
  53.5 1.8 slice.313
  55.3 1.1 slice.314
  58.1 2.9 broadcast_in_dim.6
  61.1 5.3 %div.61 = f32[192,16,256]{2,0,1:T(8,128)} reshape(f32[96,2,8,2,256]{4,1,0,3,2:T(2,128)} %broadcast_in_dim.6) | data formatting | bytes 6291456 | tf_op jit(solution)/shard_map/div | solution.py:101
  66.7 2.3 broadcast_in_dim.7
  69.0 5.0 %div.65 = f32[192,16,256]{2,0,1:T(8,128)} reshape(f32[48,4,4,4,256]{4,1,0,3,2:T(4,128)} %broadcast_in_dim.7) | data formatting | bytes 6291456 | tf_op jit(solution)/shard_map/div | solution.py:101
  74.2 5.4 %fusion = f32[256,3072]{0,1:S(1)} fusion(bf16[1536,256]{1,0:T(8,128)(2,1)S(1)} %bitcast.256, bf16[1536,4080]{0,1:T(8,128)(2,1)} %bitcast.285), kind=kOutput, calls=%fused_computation | convolution fusion | flops 2415919104 | bytes 13369344
  79.9 1.6 copy-done.3
  81.5 1.0 add_multiply_fusion
  82.4 3.5 copy.54
  86.1 3.7 %collective-permute-start.14 = (bf16[14,1,256]{2,1,0:T(2,128)(2,1)S(1)}, bf16[14,1,256]{2,1,0:T(2,128)(2,1)}, u32[]{:S(2)}, u32[]{:S(2)}) collective-permute-start(bf16[14,1,256]{2,1,0:T(2,128)(2,1)S(1)} %get-tuple-element.21), channel_id=1, source_target_pairs={{0,1},{1,2},{2,3},{3,4},{4,5},{5,6},{6,7},{8,9},{9,10},{10,11},{11... | collective-permute-start | bytes 21512 | tf_op jit(solution)/shard_map/ppermute | solution.py:18
  89.8 1.3 collective-permute-start.15
  91.2 1.3 collective-permute-start.11
  92.5 4.6 %collective-permute-start.10 = (bf16[10,1,256]{2,1,0:T(2,128)(2,1)S(1)}, bf16[10,1,256]{2,1,0:T(2,128)(2,1)S(1)}, u32[]{:S(2)}, u32[]{:S(2)}) collective-permute-start(bf16[10,1,256]{2,1,0:T(2,128)(2,1)S(1)} %get-tuple-element.15), channel_id=1, source_target_pairs={{0,1},{1,2},{2,3},{3,4},{4,5},{5,6},{6,7},{8,9},{9,10},{10,11},{11... | collective-permute-start | bytes 15368 | tf_op jit(solution)/shard_map/ppermute | solution.py:18
  97.1 0.9 convert_element_type.50
  98.1 4.5 %collective-permute-start = (bf16[1,24,256]{2,1,0:T(8,128)(2,1)S(1)}, bf16[1,24,256]{2,1,0:T(8,128)(2,1)S(1)}, u32[]{:S(2)}, u32[]{:S(2)}) collective-permute-start(bf16[1,24,256]{2,1,0:T(8,128)(2,1)S(1)} %get-tuple-element.37), channel_id=1, source_target_pairs={{0,8},{8,16},{16,24},{24,32},{32,40},{40,48},{48,56},{56,64},{64,7... | collective-permute-start | bytes 36872 | tf_op jit(solution)/shard_map/ppermute | solution.py:18
  102.6 1.9 collective-permute-start.1
  106.0 1.1 maximum_bitcast_fusion.1
  107.9 1.4 collective-permute-start.2
  109.3 4.3 %collective-permute-start.3 = (bf16[10,1,256]{2,1,0:T(2,128)(2,1)S(1)}, bf16[10,1,256]{2,1,0:T(2,128)(2,1)S(1)}, u32[]{:S(2)}, u32[]{:S(2)}) collective-permute-start(bf16[10,1,256]{2,1,0:T(2,128)(2,1)S(1)} %get-tuple-element.20), channel_id=1, source_target_pairs={{0,1},{1,2},{2,3},{3,4},{4,5},{5,6},{6,7},{8,9},{9,10},{10,11},{11... | collective-permute-start | bytes 15368 | tf_op jit(solution)/shard_map/ppermute | solution.py:18
  116.9 49.9 %reduce-scatter.5.cloned.1.call-done = f32[12,16,256]{2,1,0:T(8,128)} async-done(((f32[192,16,256]{2,1,0:T(8,128)}), f32[12,16,256]{2,1,0:T(8,128)}) %reduce-scatter.5.cloned.1.call-update) | async-done | bytes 196624 | tf_op jit(solution)/shard_map/reduce_scatter | solution.py:109
  166.8 0.9 convert_element_type.53
  168.0 4.9 %collective-permute-start.4 = (bf16[1,16,256]{2,1,0:T(8,128)(2,1)S(1)}, bf16[1,16,256]{2,1,0:T(8,128)(2,1)S(1)}, u32[]{:S(2)}, u32[]{:S(2)}) collective-permute-start(bf16[1,16,256]{2,1,0:T(8,128)(2,1)S(1)} %get-tuple-element.33), channel_id=1, source_target_pairs={{0,8},{8,16},{16,24},{24,32},{32,40},{40,48},{48,56},{56,64},{64,7... | collective-permute-start | bytes 24584 | tf_op jit(solution)/shard_map/ppermute | solution.py:18
  172.9 1.9 collective-permute-start.5
  175.1 0.9 convolution_bitcast_fusion.7
  178.0 0.9 convolution_bitcast_fusion.12
  179.9 0.9 convolution_bitcast_fusion.9
  181.2 1.0 copy-done.6
  182.2 1.7 maximum_add_fusion
  184.0 1.3 collective-permute-start.6
  185.3 4.0 %collective-permute-start.7 = (bf16[14,1,256]{2,1,0:T(2,128)(2,1)S(1)}, bf16[14,1,256]{2,1,0:T(2,128)(2,1)S(1)}, u32[]{:S(2)}, u32[]{:S(2)}) collective-permute-start(bf16[14,1,256]{2,1,0:T(2,128)(2,1)S(1)} %get-tuple-element.26), channel_id=1, source_target_pairs={{0,1},{1,2},{2,3},{3,4},{4,5},{5,6},{6,7},{8,9},{9,10},{10,11},{11... | collective-permute-start | bytes 21512 | tf_op jit(solution)/shard_map/ppermute | solution.py:18
  192.6 144.7 %all-reduce.2.cloned.1.call-done = f32[3,3,256,256]{3,2,1,0:T(8,128)} async-done(((f32[3,3,256,256]{3,2,1,0:T(8,128)}), f32[3,3,256,256]{3,2,1,0:T(8,128)}) %all-reduce.2.cloned.1.call-update) | async-done | bytes 2359312 | tf_op jit(solution)/shard_map/psum | solution.py:122
  337.4 3.3 copy.73
  (114 shorter events, 16.3 us)
Async XLA Ops:
  7.2 50.2 %copy-start = (bf16[8,192,256]{2,1,0:T(8,128)(2,1)S(1)}, bf16[8,192,256]{2,1,0:T(8,128)(2,1)}, u32[]{:S(2)}) copy-start(bf16[8,192,256]{2,1,0:T(8,128)(2,1)} %param.6) | copy-start | bytes 2359300
  7.2 4.7 %copy-start.2 = (bf16[192,16,256]{2,1,0:T(8,128)(2,1)S(1)}, bf16[192,16,256]{2,1,0:T(8,128)(2,1)}, u32[]{:S(2)}) copy-start(bf16[192,16,256]{2,1,0:T(8,128)(2,1)} %param.7) | copy-start | bytes 4718596
  7.2 90.0 %reduce-scatter.3.cloned.1.call-start = ((), (), s32[]{:S(2)}) async-start(), calls=%async_computation.2 | async-start | bytes 1769472 | tf_op jit(solution)/shard_map/reduce_scatter | solution.py:102
  28.2 2.8 copy-start.7
  40.3 0.9 copy-start.9
  40.3 7.4 %copy-start.8 = (bf16[8,24,256]{2,1,0:T(8,128)(2,1)S(1)}, bf16[8,24,256]{2,1,0:T(8,128)(2,1)}, u32[]{:S(2)}) copy-start(bf16[8,24,256]{2,1,0:T(8,128)(2,1)} %param.9) | copy-start | bytes 294916
  40.3 126.4 %reduce-scatter.5.cloned.1.call-start = ((), (), s32[]{:S(2)}) async-start(), calls=%async_computation.3 | async-start | bytes 3342336 | tf_op jit(solution)/shard_map/reduce_scatter | solution.py:109
  41.2 44.8 %collective-permute-start.12 = (bf16[1,16,256]{2,1,0:T(8,128)(2,1)S(1)}, bf16[1,16,256]{2,1,0:T(8,128)(2,1)S(1)}, u32[]{:S(2)}, u32[]{:S(2)}) collective-permute-start(bf16[1,16,256]{2,1,0:T(8,128)(2,1)S(1)} %get-tuple-element.28), channel_id=1, source_target_pairs={{0,8},{8,16},{16,24},{24,32},{32,40},{40,48},{48,56},{56,64},{64,7... | collective-permute-start | bytes 24584 | tf_op jit(solution)/shard_map/ppermute | solution.py:18
  45.8 40.2 %collective-permute-start.13 = (bf16[1,16,256]{2,1,0:T(8,128)(2,1)S(1)}, bf16[1,16,256]{2,1,0:T(8,128)(2,1)S(1)}, u32[]{:S(2)}, u32[]{:S(2)}) collective-permute-start(bf16[1,16,256]{2,1,0:T(8,128)(2,1)S(1)} %get-tuple-element.27), channel_id=1, source_target_pairs={{8,0},{16,8},{24,16},{32,24},{40,32},{48,40},{56,48},{64,56},{72,6... | collective-permute-start | bytes 24584 | tf_op jit(solution)/shard_map/ppermute | solution.py:20
  47.7 43.4 %collective-permute-start.8 = (bf16[1,24,256]{2,1,0:T(8,128)(2,1)S(1)}, bf16[1,24,256]{2,1,0:T(8,128)(2,1)S(1)}, u32[]{:S(2)}, u32[]{:S(2)}) collective-permute-start(bf16[1,24,256]{2,1,0:T(8,128)(2,1)S(1)} %get-tuple-element.30), channel_id=1, source_target_pairs={{0,8},{8,16},{16,24},{24,32},{32,40},{40,48},{48,56},{56,64},{64,7... | collective-permute-start | bytes 36872 | tf_op jit(solution)/shard_map/ppermute | solution.py:18
  51.4 39.8 %collective-permute-start.9 = (bf16[1,24,256]{2,1,0:T(8,128)(2,1)S(1)}, bf16[1,24,256]{2,1,0:T(8,128)(2,1)S(1)}, u32[]{:S(2)}, u32[]{:S(2)}) collective-permute-start(bf16[1,24,256]{2,1,0:T(8,128)(2,1)S(1)} %get-tuple-element.29), channel_id=1, source_target_pairs={{8,0},{16,8},{24,16},{32,24},{40,32},{48,40},{56,48},{64,56},{72,6... | collective-permute-start | bytes 36872 | tf_op jit(solution)/shard_map/ppermute | solution.py:20
  74.2 5.7 %copy-start.4 = (f32[192,16,256]{2,0,1:T(8,128)S(1)}, f32[192,16,256]{2,0,1:T(8,128)}, u32[]{:S(2)}) copy-start(f32[192,16,256]{2,0,1:T(8,128)} %div.65) | copy-start | bytes 9437188
  79.6 1.9 copy-start.3
  85.9 251.4 %all-reduce.2.cloned.1.call-start = ((), (), s32[]{:S(2)}) async-start(), calls=%async_computation.4 | async-start | bytes 4718592 | tf_op jit(solution)/shard_map/psum | solution.py:122
  86.0 19.2 %copy-start.11 = (bf16[14,16,256]{2,1,0:T(8,128)(2,1)}, bf16[14,16,256]{2,1,0:T(8,128)(2,1)S(1)}, u32[]{:S(2)}) copy-start(bf16[14,16,256]{2,1,0:T(8,128)(2,1)S(1)} %constant_dynamic-update-slice_fusion.3) | copy-start | bytes 344068
  86.1 89.9 %collective-permute-start.14 = (bf16[14,1,256]{2,1,0:T(2,128)(2,1)S(1)}, bf16[14,1,256]{2,1,0:T(2,128)(2,1)}, u32[]{:S(2)}, u32[]{:S(2)}) collective-permute-start(bf16[14,1,256]{2,1,0:T(2,128)(2,1)S(1)} %get-tuple-element.21), channel_id=1, source_target_pairs={{0,1},{1,2},{2,3},{3,4},{4,5},{5,6},{6,7},{8,9},{9,10},{10,11},{11... | collective-permute-start | bytes 21512 | tf_op jit(solution)/shard_map/ppermute | solution.py:18
  89.8 85.2 %collective-permute-start.15 = (bf16[14,1,256]{2,1,0:T(2,128)(2,1)S(1)}, bf16[14,1,256]{2,1,0:T(2,128)(2,1)}, u32[]{:S(2)}, u32[]{:S(2)}) collective-permute-start(bf16[14,1,256]{2,1,0:T(2,128)(2,1)S(1)} %get-tuple-element.22), channel_id=1, source_target_pairs={{1,0},{2,1},{3,2},{4,3},{5,4},{6,5},{7,6},{9,8},{10,9},{11,10},{12... | collective-permute-start | bytes 21512 | tf_op jit(solution)/shard_map/ppermute | solution.py:20
  91.2 11.4 %collective-permute-start.11 = (bf16[10,1,256]{2,1,0:T(2,128)(2,1)S(1)}, bf16[10,1,256]{2,1,0:T(2,128)(2,1)S(1)}, u32[]{:S(2)}, u32[]{:S(2)}) collective-permute-start(bf16[10,1,256]{2,1,0:T(2,128)(2,1)S(1)} %get-tuple-element.16), channel_id=1, source_target_pairs={{1,0},{2,1},{3,2},{4,3},{5,4},{6,5},{7,6},{9,8},{10,9},{11,10},{12... | collective-permute-start | bytes 15368 | tf_op jit(solution)/shard_map/ppermute | solution.py:20
  92.5 12.5 %collective-permute-start.10 = (bf16[10,1,256]{2,1,0:T(2,128)(2,1)S(1)}, bf16[10,1,256]{2,1,0:T(2,128)(2,1)S(1)}, u32[]{:S(2)}, u32[]{:S(2)}) collective-permute-start(bf16[10,1,256]{2,1,0:T(2,128)(2,1)S(1)} %get-tuple-element.15), channel_id=1, source_target_pairs={{0,1},{1,2},{2,3},{3,4},{4,5},{5,6},{6,7},{8,9},{9,10},{10,11},{11... | collective-permute-start | bytes 15368 | tf_op jit(solution)/shard_map/ppermute | solution.py:18
  98.1 9.7 %collective-permute-start = (bf16[1,24,256]{2,1,0:T(8,128)(2,1)S(1)}, bf16[1,24,256]{2,1,0:T(8,128)(2,1)S(1)}, u32[]{:S(2)}, u32[]{:S(2)}) collective-permute-start(bf16[1,24,256]{2,1,0:T(8,128)(2,1)S(1)} %get-tuple-element.37), channel_id=1, source_target_pairs={{0,8},{8,16},{16,24},{24,32},{32,40},{40,48},{48,56},{56,64},{64,7... | collective-permute-start | bytes 36872 | tf_op jit(solution)/shard_map/ppermute | solution.py:18
  102.6 5.2 %collective-permute-start.1 = (bf16[1,24,256]{2,1,0:T(8,128)(2,1)S(1)}, bf16[1,24,256]{2,1,0:T(8,128)(2,1)S(1)}, u32[]{:S(2)}, u32[]{:S(2)}) collective-permute-start(bf16[1,24,256]{2,1,0:T(8,128)(2,1)S(1)} %get-tuple-element.38), channel_id=1, source_target_pairs={{8,0},{16,8},{24,16},{32,24},{40,32},{48,40},{56,48},{64,56},{72,6... | collective-permute-start | bytes 36872 | tf_op jit(solution)/shard_map/ppermute | solution.py:20
  107.5 6.1 %copy-start.5 = (bf16[3,3,256,256]{3,2,1,0:T(8,128)(2,1)S(1)}, bf16[3,3,256,256]{3,2,1,0:T(8,128)(2,1)}, u32[]{:S(2)}) copy-start(bf16[3,3,256,256]{3,2,1,0:T(8,128)(2,1)} %param.11) | copy-start | bytes 3538948
  107.9 6.0 %collective-permute-start.2 = (bf16[10,1,256]{2,1,0:T(2,128)(2,1)S(1)}, bf16[10,1,256]{2,1,0:T(2,128)(2,1)S(1)}, u32[]{:S(2)}, u32[]{:S(2)}) collective-permute-start(bf16[10,1,256]{2,1,0:T(2,128)(2,1)S(1)} %get-tuple-element.19), channel_id=1, source_target_pairs={{1,0},{2,1},{3,2},{4,3},{5,4},{6,5},{7,6},{9,8},{10,9},{11,10},{12... | collective-permute-start | bytes 15368 | tf_op jit(solution)/shard_map/ppermute | solution.py:20
  109.3 5.1 %collective-permute-start.3 = (bf16[10,1,256]{2,1,0:T(2,128)(2,1)S(1)}, bf16[10,1,256]{2,1,0:T(2,128)(2,1)S(1)}, u32[]{:S(2)}, u32[]{:S(2)}) collective-permute-start(bf16[10,1,256]{2,1,0:T(2,128)(2,1)S(1)} %get-tuple-element.20), channel_id=1, source_target_pairs={{0,1},{1,2},{2,3},{3,4},{4,5},{5,6},{6,7},{8,9},{9,10},{10,11},{11... | collective-permute-start | bytes 15368 | tf_op jit(solution)/shard_map/ppermute | solution.py:18
  115.4 52.3 %copy-start.10 = (bf16[12,16,256]{2,1,0:T(8,128)(2,1)S(1)}, bf16[12,16,256]{2,1,0:T(8,128)(2,1)}, u32[]{:S(2)}) copy-start(bf16[12,16,256]{2,1,0:T(8,128)(2,1)} %param.10) | copy-start | bytes 294916
  116.0 59.0 %copy-start.12 = (bf16[14,16,256]{2,1,0:T(8,128)(2,1)S(1)}, bf16[14,16,256]{2,1,0:T(8,128)(2,1)}, u32[]{:S(2)}) copy-start(bf16[14,16,256]{2,1,0:T(8,128)(2,1)} %copy-done.11) | copy-start | bytes 344068
  168.0 16.0 %collective-permute-start.4 = (bf16[1,16,256]{2,1,0:T(8,128)(2,1)S(1)}, bf16[1,16,256]{2,1,0:T(8,128)(2,1)S(1)}, u32[]{:S(2)}, u32[]{:S(2)}) collective-permute-start(bf16[1,16,256]{2,1,0:T(8,128)(2,1)S(1)} %get-tuple-element.33), channel_id=1, source_target_pairs={{0,8},{8,16},{16,24},{24,32},{32,40},{40,48},{48,56},{56,64},{64,7... | collective-permute-start | bytes 24584 | tf_op jit(solution)/shard_map/ppermute | solution.py:18
  172.9 11.0 %collective-permute-start.5 = (bf16[1,16,256]{2,1,0:T(8,128)(2,1)S(1)}, bf16[1,16,256]{2,1,0:T(8,128)(2,1)S(1)}, u32[]{:S(2)}, u32[]{:S(2)}) collective-permute-start(bf16[1,16,256]{2,1,0:T(8,128)(2,1)S(1)} %get-tuple-element.34), channel_id=1, source_target_pairs={{8,0},{16,8},{24,16},{32,24},{40,32},{48,40},{56,48},{64,56},{72,6... | collective-permute-start | bytes 24584 | tf_op jit(solution)/shard_map/ppermute | solution.py:20
  181.0 1.1 copy-start.6
  184.0 5.5 %collective-permute-start.6 = (bf16[14,1,256]{2,1,0:T(2,128)(2,1)S(1)}, bf16[14,1,256]{2,1,0:T(2,128)(2,1)S(1)}, u32[]{:S(2)}, u32[]{:S(2)}) collective-permute-start(bf16[14,1,256]{2,1,0:T(2,128)(2,1)S(1)} %get-tuple-element.25), channel_id=1, source_target_pairs={{1,0},{2,1},{3,2},{4,3},{5,4},{6,5},{7,6},{9,8},{10,9},{11,10},{12... | collective-permute-start | bytes 21512 | tf_op jit(solution)/shard_map/ppermute | solution.py:20
  185.3 4.8 %collective-permute-start.7 = (bf16[14,1,256]{2,1,0:T(2,128)(2,1)S(1)}, bf16[14,1,256]{2,1,0:T(2,128)(2,1)S(1)}, u32[]{:S(2)}, u32[]{:S(2)}) collective-permute-start(bf16[14,1,256]{2,1,0:T(2,128)(2,1)S(1)} %get-tuple-element.26), channel_id=1, source_target_pairs={{0,1},{1,2},{2,3},{3,4},{4,5},{5,6},{6,7},{8,9},{9,10},{10,11},{11... | collective-permute-start | bytes 21512 | tf_op jit(solution)/shard_map/ppermute | solution.py:18
  337.4 3.3 copy-start.1
Sparse Core Ops, SparseCore 0:
  40.5 39.0 reduce-scatter.2
  86.0 80.6 reduce-scatter.4
  184.0 153.2 all-reduce.1
where the time goes:
time: 349 us; the launch traced here: 347 us
  waiting for transfers between devices  196 us (56%)
  starting transfers between devices  47.5 us (14%)
  local copies, waits for them, and re-layouts  38.9 us (11%)
  matrix products  32.2 us (9%)
  other arithmetic  18.1 us (5%)
  between operations  14.6 us (4%)
    psum x1, waiting for transfers between devices, body(): weight_grad = lax.psum(local_weight, ('pb', 'ka'))  145 us
    reduce_scatter x1, waiting for transfers between devices, body(): lax.psum_scatter((fine_term + coarse_sum) * norm_scale, 'pb', scatter_dim...  49.9 us
    ppermute x8, starting transfers between devices, padded(): lax.ppermute(tail, axis, [(i, (i + 1) % count) for i in range(ends)])  34.2 us
    ppermute x8, starting transfers between devices, padded(): lax.ppermute(head, axis, [((i + 1) % count, i) for i in range(ends)])  13.2 us
    dot_general x4, matrix products, body(): jnp.dot(grad_block, ordered, preferred_element_type=jnp.float32)  12 us
    div x2, local copies, waits for them, and re-layouts, body(): coarse_sum = coarse_sum + spread / 4.0 ** level_index  10.2 us
    reduce_sum x3, other arithmetic, pool_levels(): pooled = strip_float.reshape(cell_cols // factor, factor, key_rows // fac...  9.77 us
    unnamed x32, local copies, waits for them, and re-layouts  8.44 us
  transfers between devices with their start and end apart: 19, of which 4 were waited for; matrix products, arithmetic and copies ran while one was open for 14% of the time, Pallas kernels for 0%

commit v1 on v0

v1 whole, which is shorter than its diff:
```python
import jax
import jax.numpy as jnp
from jax import lax
from jax.experimental import pallas as pl
from jax.experimental.pallas import tpu as pltpu
from jax.sharding import PartitionSpec as P

BF = jnp.bfloat16
F32 = jnp.float32
MESH = pl.DeviceIdType.MESH
CELLS = 4080
QN = 1536
QP = 384
ST = 384
NT = (((1,), (1,)), ((), ()))


def dot(a, b):
    return jnp.dot(a, b, preferred_element_type=F32)


def dot_nt(a, b):
    return lax.dot_general(a, b, NT, preferred_element_type=F32)


def div(v, d):
    return lax.shift_right_logical(v * (-(-(1 << 20) // d)), 20)


def col(n):
    return lax.broadcasted_iota(jnp.int32, (n, 1), 0)


def row(n):
    return lax.broadcasted_iota(jnp.int32, (1, n), 1)


def select(src, n, value=1.0):
    wide = lax.broadcasted_iota(jnp.int32, (src.shape[0], n), 1)
    return jnp.where(wide == src, value, 0.0).astype(BF)


def pick(key, n, value):
    tall = lax.broadcasted_iota(jnp.int32, (n, key.shape[1]), 0)
    return jnp.where(tall == key, value, 0.0).astype(BF)


def kernel(
    g_hbm, q_hbm, k_hbm, qi_hbm, ki_hbm, cw_hbm,
    qg_out, kg_out, w_out,
    g, qv, kv, cw, pool, pool_t, mid, fine, kt, qt,
    c0s, c0r, s1, r1, s2, r2, s3, r3,
    stage, colp, rowp, padt, win_t, grad, wacc,
    a0s, a0r, w1, a1s, a1r, a2s, a2r, a3, wfull, ogs,
    in_sem, send_sem, recv_sem,
):
    pb, ka = lax.axis_index("pb"), lax.axis_index("ka")
    core = pb % 2
    cy = (pb // 2) % 4
    zh = pb // 8
    cx = ka % 4
    zl = ka // 4
    cz = zh * 2 + zl

    def device(x, y, z, c):
        return {"pb": ((z // 2) * 4 + y) * 2 + c, "ka": (z % 2) * 4 + x}

    def shift(dim, d):
        return device(
            (cx + d) % 4 if dim == 0 else cx,
            (cy + d) % 4 if dim == 1 else cy,
            (cz + d) % 4 if dim == 2 else cz,
            core,
        )

    other_core = device(cx, cy, cz, 1 - core)
    pb_up = {"pb": (pb + 15) % 16, "ka": ka}
    pb_down = {"pb": (pb + 1) % 16, "ka": ka}
    ka_up = {"pb": pb, "ka": (ka + 7) % 8}
    ka_down = {"pb": pb, "ka": (ka + 1) % 8}

    counter = [0]

    def send(src, dst, dev):
        n = counter[0]
        counter[0] += 1
        copy = pltpu.make_async_remote_copy(
            src_ref=src, dst_ref=dst, send_sem=send_sem.at[n], recv_sem=recv_sem.at[n],
            device_id=dev, device_id_type=MESH,
        )
        copy.start()
        pending.append(copy)
        return copy

    pending = []
    loads = []

    def load(src, dst):
        copy = pltpu.make_async_copy(src, dst, in_sem.at[len(loads)])
        copy.start()
        loads.append(copy)
        return copy

    ld_k = load(k_hbm, kv)
    ld_q = load(q_hbm, qv)
    ld_gc = load(g_hbm.at[pl.ds(3072, 1008)], g.at[pl.ds(3072, 1008)])
    ld_img = [load(qi_hbm, stage.at[0, pl.ds(0, 192)]), load(ki_hbm, stage.at[1, pl.ds(0, 192)])]
    ld_g = [load(g_hbm.at[pl.ds(768 * i, 768)], g.at[pl.ds(768 * i, 768)]) for i in range(4)]
    ld_cw = load(cw_hbm, cw)

    barrier = pltpu.get_barrier_semaphore()
    partners = [other_core, pb_up, pb_down, ka_up, ka_down]
    partners += [shift(dim, d) for dim in range(3) for d in (1, 2, 3)]
    for partner in partners:
        pl.semaphore_signal(barrier, inc=1, device_id=partner, device_id_type=MESH)

    for s in range(4):
        stage[s, 288:ST, :] = jnp.zeros((ST - 288, 256), BF)
    g[CELLS:4096, :] = jnp.zeros((4096 - CELLS, QN), BF)
    pool[CELLS:4096, :] = jnp.zeros((4096 - CELLS, 256), BF)

    rows_of = (8, 12, 8, 12)
    cols_of = (24, 16, 24, 16)

    def tile_index(s, i, j):
        return j * 12 + i if s == 3 else i * cols_of[s] + j

    def halo_cols(s):
        n_r, n_c = rows_of[s], cols_of[s]
        v = col(32)
        i = v & 15
        src = jnp.where(v < 16, tile_index(s, i, 0), tile_index(s, i, n_c - 1))
        src = jnp.where(i < n_r, src, -1)
        colp[s] = dot(select(src, 192), stage[s, 0:192, :]).astype(BF)
        return [
            send(colp.at[s, pl.ds(0, 16)], stage.at[s, pl.ds(208, 16)], ka_up),
            send(colp.at[s, pl.ds(16, 16)], stage.at[s, pl.ds(192, 16)], ka_down),
        ]

    def halo_rows(s):
        n_r, n_c = rows_of[s], cols_of[s]
        v = col(64)
        j = (v & 31) - 1
        i = jnp.where(v < 32, 0, n_r - 1)
        src = tile_index(s, i, j)
        src = jnp.where(j < 0, jnp.where(ka == 0, -1, 192 + i), src)
        src = jnp.where(j == n_c, jnp.where(ka == 7, -1, 208 + i), src)
        src = jnp.where(j > n_c, -1, src)
        rowp[s] = dot(select(src, 224), stage[s, 0:224, :]).astype(BF)
        return [
            send(rowp.at[s, pl.ds(0, 32)], stage.at[s, pl.ds(256, 32)], pb_up),
            send(rowp.at[s, pl.ds(32, 32)], stage.at[s, pl.ds(224, 32)], pb_down),
        ]

    def padded(s):
        n_r, n_c = rows_of[s], cols_of[s]
        v = col(QP)
        ip = div(v, n_c + 2)
        jp = v - ip * (n_c + 2)
        i, j = ip - 1, jp - 1
        src = tile_index(s, i, j)
        src = jnp.where(j < 0, jnp.where(ka == 0, -1, 192 + i), src)
        src = jnp.where(j == n_c, jnp.where(ka == 7, -1, 208 + i), src)
        src = jnp.where(i < 0, jnp.where(pb == 0, -1, 224 + jp), src)
        src = jnp.where(i == n_r, jnp.where(pb == 15, -1, 256 + jp), src)
        src = jnp.where(i > n_r, -1, src)
        return dot(select(src, ST), stage[s]).astype(BF)

    def tap_offset(s, rs, cs):
        pitch = cols_of[s] + 2
        return cs * pitch + rs if s % 2 else rs * pitch + cs

    def pool_keys():
        o = col(256)
        perm = select((o & 15) * 16 + lax.shift_right_logical(o, 4), 256)
        for b in range(12):
            block = dot(perm, kv[256 * b:256 * b + 256, :]).astype(BF)
            for r in range(16):
                pool[192 * r + 16 * b:192 * r + 16 * b + 16, :] = block[16 * r:16 * r + 16, :]
        k = row(512)
        key = lax.shift_right_logical(k & 15, 1) * 16 + lax.shift_right_logical(k, 5)
        mean = pick(key, 128, 0.25)
        for b in range(6):
            block = dot(mean, kv[512 * b:512 * b + 512, :]).astype(BF)
            for r in range(8):
                at = 3072 + 96 * r + 16 * b
                pool[at:at + 16, :] = block[16 * r:16 * r + 16, :]
        k = row(1024)
        key = lax.shift_right_logical(k & 15, 2) * 16 + lax.shift_right_logical(k, 6)
        mean = pick(key, 64, 0.0625)
        for b in range(3):
            block = dot(mean, kv[1024 * b:1024 * b + 1024, :]).astype(BF)
            for r in range(4):
                at = 3840 + 48 * r + 16 * b
                pool[at:at + 16, :] = block[16 * r:16 * r + 16, :]
        k = row(3072)
        key = (lax.shift_right_logical(k, 3) & 1) * 24 + lax.shift_right_logical(k, 7)
        pool[4032:4080, :] = dot(pick(key, 48, 0.015625), kv[...]).astype(BF)
        o = col(256)
        eye = select(o, 256)
        for b in range(16):
            pool_t[:, 256 * b:256 * b + 256] = dot_nt(eye, pool[256 * b:256 * b + 256, :]).astype(BF)

    def coarse_levels():
        c = dot(g[3072:4080, :], qv[...])
        l3 = (c[960:1008, :] * (1.0 / 64.0)).astype(BF)
        v = col(192)
        r = div(v, 48)
        src = lax.shift_right_logical(r, 1) * 24 + lax.shift_right_logical(v - r * 48, 1)
        l2 = (c[768:960, :] * (1.0 / 16.0) + dot(select(src, 48), l3)).astype(BF)
        v = col(768)
        r = div(v, 96)
        src = lax.shift_right_logical(r, 1) * 48 + lax.shift_right_logical(v - r * 96, 1)
        mid[...] = (c[0:768, :] * 0.25 + dot(select(src, 192), l2)).astype(BF)

    def key_chunk(i):
        v = col(768)
        r = div(v, 192)
        src = lax.shift_right_logical(r, 1) * 96 + lax.shift_right_logical(v - r * 192, 1)
        fine[...] = dot(g[768 * i:768 * i + 768, :], qv[...]) + dot(
            select(src, 192), mid[192 * i:192 * i + 192, :]
        )
        for t in range(8):
            for p in range(2):
                for r in range(4):
                    at = 192 * r + 24 * t + 12 * p
                    kt[i, p, t, 12 * r:12 * r + 12, :] = fine[at:at + 12, :]
        c0s[i] = kt[i, 1 - core].astype(BF)
        return send(c0s.at[i], c0r.at[i], other_core)

    def query_chunk(i):
        part = dot(pool_t[...], g[:, 384 * i:384 * i + 384])
        part = jnp.transpose(part)
        for hh in range(2):
            for k in range(8):
                at = 192 * hh + 24 * k
                qt[i, k, 24 * hh:24 * hh + 24, :] = part[at:at + 24, :]

    def along(u):
        return (1, cy, zh) if u < 4 else (0, cx, zl)

    def part_of(u, g_, n, c):
        lanes = slice(128 * c, 128 * c + 128)
        tile = g_ * 4 + n
        if u < 4:
            return kt[u, core, tile, :, lanes]
        return qt[u - 4, tile, :, lanes]

    def mates(u):
        dim, n, _ = along(u)
        flip = n + 1 - 2 * (n % 2)
        mirror = 3 - n
        return ((flip, mirror), (mirror, flip))

    def ring(u, n):
        dim = along(u)[0]
        return device(n if dim == 0 else cx, n if dim == 1 else cy, cz, core)

    def last_mate(u):
        if u < 4:
            return device(cx, cy, (1 - zh) * 2 + zl, core)
        return device(cx, cy, zh * 2 + (1 - zl), core)

    flight = {}

    def step1(u):
        out = []
        for c in range(2):
            first, _ = mates(u)[c]
            flip = first + 1 - 2 * (first % 2)
            beyond = (3 - first) if c == 0 else flip
            for j in range(4):
                n = first if j < 2 else beyond
                s1[u, c, j] = part_of(u, j % 2, n, c).astype(BF)
            out.append(send(s1.at[u, c], r1.at[u, c], ring(u, first)))
        flight[u, 1] = out

    def step2(u):
        out = []
        for c in range(2):
            flight[u, 1][c].wait_recv()
            _, second = mates(u)[c]
            for j in range(2):
                s2[u, c, j] = (part_of(u, j, second, c) + r1[u, c, 2 + j].astype(F32)).astype(BF)
            out.append(send(s2.at[u, c], r2.at[u, c], ring(u, second)))
        flight[u, 2] = out

    def step3(u):
        out = []
        _, n, z = along(u)
        for c in range(2):
            flight[u, 2][c].wait_recv()
            far = part_of(u, 1 - z, n, c) + r1[u, c, 1 - z].astype(F32) + r2[u, c, 1 - z].astype(F32)
            s3[u, c] = far.astype(BF)
            out.append(send(s3.at[u, c], r3.at[u, c], last_mate(u)))
        flight[u, 3] = out

    def finish(u):
        _, n, z = along(u)
        s = 3 if u < 4 else 2
        at = 48 * (u % 4)
        for c in range(2):
            flight[u, 3][c].wait_recv()
            total = part_of(u, z, n, c) + r1[u, c, z].astype(F32) + r2[u, c, z].astype(F32)
            total = (total + r3[u, c].astype(F32)) * 0.0625
            stage[s, at:at + 48, 128 * c:128 * c + 128] = total.astype(BF)

    def core_step(u):
        flight[u, 0].wait_recv()
        kt[u, core] = kt[u, core] + c0r[u].astype(F32)
        step1(u)

    def image_windows(s):
        o = col(256)
        padt[s] = dot_nt(select(o, 256), padded(s)).astype(BF)
        v = col(192)
        if s == 0:
            i = div(v, 24)
            f = i * 26 + (v - i * 24)
        else:
            j = div(v, 12)
            f = (v - j * 12) * 18 + j
        for rs in range(3):
            for cs in range(3):
                sel = select(f + tap_offset(s, rs, cs), QP)
                win_t[s, rs * 3 + cs] = dot_nt(padt[s], sel).astype(BF)

    def weight_part(s, first):
        for t in range(9):
            term = dot(win_t[s, t], stage[s + 2, 0:192, :])
            wacc[256 * t:256 * t + 256, :] = term if first else wacc[256 * t:256 * t + 256, :] + term

    def input_grad(s, slot):
        pad = padded(s)
        v = col(192)
        if s == 2:
            i = div(v, 24)
            f = i * 26 + (v - i * 24)
        else:
            f = lax.shift_right_logical(v, 4) * 18 + (v & 15)
        acc = jnp.zeros((192, 256), F32)
        for rs in range(3):
            for cs in range(3):
                sel = select(f + tap_offset(s, 2 - rs, 2 - cs), QP)
                win = dot(sel, pad).astype(BF)
                at = 256 * (rs * 3 + cs)
                acc = acc + dot_nt(win, cw[at:at + 256, :])
        ogs[slot] = acc.astype(BF)

    ld_k.wait()
    pool_keys()
    for c in ld_img:
        c.wait()
    pl.semaphore_wait(barrier, len(partners))
    hc = [halo_cols(0), halo_cols(1)]
    ld_q.wait()
    ld_gc.wait()
    coarse_levels()
    hr = []
    for slot in range(12):
        if slot < 4:
            ld_g[slot].wait()
            flight[slot, 0] = key_chunk(slot)
        elif slot < 8:
            query_chunk(slot - 4)
            step1(slot)
        if slot == 2:
            for s in range(2):
                for c in hc[s]:
                    c.wait_recv()
                hr.append(halo_rows(s))
        if slot == 8:
            for s in range(2):
                for c in hr[s]:
                    c.wait_recv()
                image_windows(s)
        for u in range(4):
            if slot == u + 1:
                core_step(u)
            if slot == u + 3:
                step2(u)
            if slot == u + 5:
                step3(u)
            v = u + 4
            if slot == v + 2:
                step2(v)
            if slot == v + 4:
                step3(v)
        if slot == 10:
            for u in range(4):
                finish(u)
            hk = halo_cols(3)
            weight_part(1, True)
    for u in range(4, 8):
        finish(u)
    hq = halo_cols(2)
    weight_part(0, False)

    for h in range(2):
        for j in range(3):
            for n in range(4):
                at = 768 * j + 192 * n
                w1[h, j, n] = wacc[at:at + 192, 128 * h:128 * h + 128]
    a0s[...] = w1[1 - core].astype(BF)
    c0 = send(a0s, a0r, other_core)
    for c in hk:
        c.wait_recv()
    hk = halo_rows(3)
    ld_cw.wait()
    c0.wait_recv()
    w1[core] = w1[core] + a0r[...].astype(F32)
    coords = (cx, cy, cz)
    a1s[...] = w1[core].astype(BF)
    f1 = []
    for j in range(3):
        n = coords[j]
        f1.append([
            send(a1s.at[j, (n + d) % 4], a1r.at[j, d - 1], shift(j, d)) for d in (1, 2, 3)
        ])
    for c in hq:
        c.wait_recv()
    hq = halo_rows(2)
    for c in hk:
        c.wait_recv()
    input_grad(3, 1)
    kg_copy = load(ogs.at[1], kg_out)
    f2 = []
    x1 = []
    for j in range(3):
        for c in f1[j]:
            c.wait_recv()
        x = w1[core, j, coords[j]]
        for d in range(3):
            x = x + a1r[j, d].astype(F32)
        w1[core, j, coords[j]] = x
        for n in range(4):
            a2s[j, n] = x[48 * n:48 * n + 48, :].astype(BF)
        b = (j + 1) % 3
        f2.append([
            send(a2s.at[j, (coords[b] + d) % 4], a2r.at[j, d - 1], shift(b, d)) for d in (1, 2, 3)
        ])
    for c in hq:
        c.wait_recv()
    input_grad(2, 0)
    qg_copy = load(ogs.at[0], qg_out)
    f3 = []
    for j in range(3):
        for c in f2[j]:
            c.wait_recv()
        b, e = (j + 1) % 3, (j + 2) % 3
        at = pl.multiple_of(coords[b] * 48, 48)
        y = w1[core, j, coords[j], pl.ds(at, 48), :]
        for d in range(3):
            y = y + a2r[j, d].astype(F32)
        a3[j, 0] = y.astype(BF)
        f3.append([send(a3.at[j, 0], a3.at[j, d], shift(e, d)) for d in (1, 2, 3)])
    f4 = []
    for j in range(3):
        for c in f3[j]:
            c.wait_recv()
        b, e = (j + 1) % 3, (j + 2) % 3
        y = jnp.zeros((48, 128), F32)
        for k in range(4):
            y = y + a3[j, (coords[e] + 4 - k) % 4].astype(F32)
        mine = wfull.at[core, j, coords[j], coords[b]]
        mine[...] = y.astype(BF)
        f4.append([send(mine, mine, shift(b, d)) for d in (1, 2, 3)])
    f5 = []
    for j in range(3):
        for c in f4[j]:
            c.wait_recv()
        mine = wfull.at[core, j, coords[j]]
        f5.append([send(mine, mine, shift(j, d)) for d in (1, 2, 3)])
    f6 = []
    for j in range(3):
        for c in f5[j]:
            c.wait_recv()
        mine = wfull.at[core, j]
        f6.append(send(mine, mine, other_core))
    for c in f6:
        c.wait_recv()
    w_copy = load(wfull, w_out)
    for c in pending:
        c.wait_send()
    for c in (kg_copy, qg_copy, w_copy):
        c.wait()


def vmem(*shape, dtype=BF):
    return pltpu.VMEM(shape, dtype)


def body(query_features, key_features, pyramid_grad, query_image, key_image, conv_weight):
    cells = jnp.transpose(pyramid_grad.reshape(QN, CELLS))
    anywhere = pl.BlockSpec(memory_space=pl.ANY)
    qg, kg, w = pl.pallas_call(
        kernel,
        out_shape=(
            jax.ShapeDtypeStruct((192, 256), BF),
            jax.ShapeDtypeStruct((192, 256), BF),
            jax.ShapeDtypeStruct((2, 3, 4, 4, 48, 128), BF),
        ),
        in_specs=[anywhere] * 6,
        out_specs=[anywhere] * 3,
        scratch_shapes=[
            vmem(4096, QN), vmem(QN, 256), vmem(3072, 256), vmem(2304, 256),
            vmem(4096, 256), vmem(256, 4096), vmem(768, 256), vmem(768, 256, dtype=F32),
            vmem(4, 2, 8, 48, 256, dtype=F32), vmem(4, 8, 48, 256, dtype=F32),
            vmem(4, 8, 48, 256), vmem(4, 8, 48, 256),
            vmem(8, 2, 4, 48, 128), vmem(8, 2, 4, 48, 128),
            vmem(8, 2, 2, 48, 128), vmem(8, 2, 2, 48, 128),
            vmem(8, 2, 48, 128), vmem(8, 2, 48, 128),
            vmem(4, ST, 256), vmem(4, 32, 256), vmem(4, 64, 256),
            vmem(2, 256, QP), vmem(2, 9, 256, 192), vmem(8, 128), vmem(2304, 256, dtype=F32),
            vmem(3, 4, 192, 128), vmem(3, 4, 192, 128), vmem(2, 3, 4, 192, 128, dtype=F32),
            vmem(3, 4, 192, 128), vmem(3, 3, 192, 128),
            vmem(3, 4, 48, 128), vmem(3, 3, 48, 128), vmem(3, 4, 48, 128),
            vmem(2, 3, 4, 4, 48, 128), vmem(2, 192, 256),
            pltpu.SemaphoreType.DMA((16,)),
            pltpu.SemaphoreType.DMA((128,)),
            pltpu.SemaphoreType.DMA((128,)),
        ],
        compiler_params=pltpu.CompilerParams(
            collective_id=0, has_side_effects=True, vmem_limit_bytes=63000 * 1024
        ),
    )(
        cells,
        query_features.reshape(QN, 256),
        key_features.reshape(3072, 256),
        query_image.reshape(192, 256),
        key_image.reshape(192, 256),
        conv_weight.reshape(2304, 256),
    )
    w = jnp.transpose(w.reshape(2, 2304, 128), (1, 0, 2)).reshape(3, 3, 256, 256)
    return qg.reshape(8, 24, 256), kg.reshape(12, 16, 256), w.astype(F32)


def solution(mesh):
    placed = (
        P("pb", None, None),
        P(None, "ka", None),
        P("pb", "ka", None),
        P("pb", "ka", None),
        P("pb", "ka", None),
        P(),
    )
    return jax.shard_map(
        body,
        mesh=mesh,
        in_specs=placed,
        out_specs=(P("pb", "ka", None), P("pb", "ka", None), P()),
        check_vma=False,
    )
```

time: 349 us -> 78.9 us (0.23)
  waiting for transfers between devices: 196 us -> 0 us
  Pallas kernels: 0 us -> 63.5 us
  starting transfers between devices: 47.5 us -> 0 us
  matrix products: 32.2 us -> 0 us
  local copies, waits for them, and re-layouts: 38.9 us -> 13.1 us
  other arithmetic: 18.1 us -> 1.42 us
  between operations: 14.6 us -> 0.67 us
    psum x1 -> x0, waiting for transfers between devices: 145 us -> none  [body(): weight_grad = lax.psum(local_weight, ('pb', 'ka'))]
    pallas_call x0 -> x1, Pallas kernels: none -> 63.5 us  [body(): pl.pallas_call(kernel, out_shape=(jax.ShapeDtypeStruct((192, 256), BF), j...]
    reduce_scatter x2 -> x0, waiting for transfers between devices: 49.9 us -> none  [the longest x1 49.9 us: body(): lax.psum_scatter((fine_term + coarse_sum) * norm_scale, 'pb', scatter_dim...]
    ppermute x16 -> x0, starting transfers between devices: 47.4 us -> none  [the longest x8 34.2 us: padded(): lax.ppermute(tail, axis, [(i, (i + 1) % count) for i in range(ends)])]
    dot_general x43 -> x0, matrix products: 26.9 us -> none  [the longest x4 12 us: body(): jnp.dot(grad_block, ordered, preferred_element_type=jnp.float32)]
    convert_element_type x3 -> x2, local copies, waits for them, and re-layouts: 0.09 us -> 11.8 us  [body(): return (qg.reshape(8, 24, 256), kg.reshape(12, 16, 256), w.astype(F32))]
    div x2 -> x0, local copies, waits for them, and re-layouts: 10.2 us -> none  [body(): coarse_sum = coarse_sum + spread / 4.0 ** level_index]
    reduce_sum x3 -> x0, other arithmetic: 9.77 us -> none  [pool_levels(): pooled = strip_float.reshape(cell_cols // factor, factor, key_rows // fac...]
  transfers between devices with their start and end apart: 19 -> 0, of which waited for: 4 -> 0; matrix products, arithmetic and copies ran while one was open for 14% -> 0% of each run, Pallas kernels for 0% -> 0%
where the time goes in v1:
time: 78.9 us; the launch traced here: 78.7 us
  Pallas kernels  63.5 us (80%)
  local copies, waits for them, and re-layouts  13.1 us (17%)
  other arithmetic  1.42 us (2%)
    pallas_call x1, Pallas kernels, body(): pl.pallas_call(kernel, out_shape=(jax.ShapeDtypeStruct((192, 256), BF), j...  63.5 us
    convert_element_type x2, local copies, waits for them, and re-layouts, body(): return (qg.reshape(8, 24, 256), kg.reshape(12, 16, 256), w.astype(F32))  11.8 us

profile of v1, /device:TPU:1, one launch (start us, length us, event | category | flops | bytes accessed | tf_op | source)
XLA Modules:
  0.0 78.7 jit_solution(17523617455660493403)
XLA Ops:
  0.6 63.5 %shard_map.85 = (bf16[192,256]{1,0:T(8,128)(2,1)}, bf16[192,256]{1,0:T(8,128)(2,1)}, bf16[2,3,4,4,48,128]{5,4,3,2,1,0:T(8,128)(2,1)}) custom-call(bf16[4080,1536]{1,0:T(8,128)(2,1)} %bitcast.15, bf16[1536,256]{1,0:T(8,128)(2,1)} %bitcast.18, bf16[3072,256]{1,0:T(8,128)(2,1)} %bitcast.16, bf16[192,256]{1,0:T(8,128)(2,1)} %bitcast.19, ...), custom_call_target="tpu_custom_call" | custom-call | tf_op jit(solution)/shard_map/pallas_call | solution.py:496
  64.2 1.4 %convert_bitcast_fusion = f32[2304,2,128]{2,0,1:T(8,128)S(1)} fusion(bf16[2,3,4,4,48,128]{5,4,3,2,1,0:T(8,128)(2,1)} %get-tuple-element.8), kind=kLoop, calls=%fused_computation | loop fusion | flops 589824 | bytes 3538944 | tf_op jit(solution)/shard_map/convert_element_type | solution.py:535
  65.6 8.9 %copy.9 = f32[2304,2,128]{2,1,0:T(2,128)S(1)} copy(f32[2304,2,128]{2,0,1:T(8,128)S(1)} %convert_bitcast_fusion) | data formatting | bytes 4718592 | tf_op jit(solution)/shard_map/convert_element_type | solution.py:535
  74.5 0.0 copy-start.1
  74.5 0.0 copy-start
  74.5 2.9 %reshape.44 = f32[3,3,256,256]{3,2,1,0:T(8,128)} reshape(f32[2304,2,128]{2,1,0:T(2,128)S(1)} %copy.9) | data formatting | bytes 4718592 | tf_op jit(solution)/shard_map/convert_element_type | solution.py:535
  77.4 0.0 copy-done.1
  77.4 0.6 copy.12
  78.1 0.0 copy-done
  78.1 0.6 copy.13
Async XLA Ops:
  74.5 3.0 %copy-start.1 = (bf16[192,256]{1,0:T(8,128)(2,1)S(1)}, bf16[192,256]{1,0:T(8,128)(2,1)}, u32[]{:S(2)}) copy-start(bf16[192,256]{1,0:T(8,128)(2,1)} %get-tuple-element.6) | copy-start | bytes 294916
  74.5 3.6 %copy-start = (bf16[192,256]{1,0:T(8,128)(2,1)S(1)}, bf16[192,256]{1,0:T(8,128)(2,1)}, u32[]{:S(2)}) copy-start(bf16[192,256]{1,0:T(8,128)(2,1)} %get-tuple-element.7) | copy-start | bytes 294916

commit v2 on v1

v2 whole, which is shorter than its diff:
```python
import jax
import jax.numpy as jnp
from jax import lax
from jax.experimental import pallas as pl
from jax.experimental.pallas import tpu as pltpu
from jax.sharding import PartitionSpec as P

BF = jnp.bfloat16
F32 = jnp.float32
MESH = pl.DeviceIdType.MESH
CELLS = 4080
QN = 1536
VMEM_BYTES = 50 * 1024 * 1024
QP = 384
ST = 384
NT = (((1,), (1,)), ((), ()))


def dot(a, b):
    return jnp.dot(a, b, preferred_element_type=F32)


def dot_nt(a, b):
    return lax.dot_general(a, b, NT, preferred_element_type=F32)


def div(v, d):
    return lax.shift_right_logical(v * (-(-(1 << 20) // d)), 20)


def col(n):
    return lax.broadcasted_iota(jnp.int32, (n, 1), 0)


def row(n):
    return lax.broadcasted_iota(jnp.int32, (1, n), 1)


def select(src, n, value=1.0):
    wide = lax.broadcasted_iota(jnp.int32, (src.shape[0], n), 1)
    return jnp.where(wide == src, value, 0.0).astype(BF)


def pick(key, n, value):
    tall = lax.broadcasted_iota(jnp.int32, (n, key.shape[1]), 0)
    return jnp.where(tall == key, value, 0.0).astype(BF)


def kernel(
    g_hbm, q_hbm, k_hbm, qi_hbm, ki_hbm, cw_hbm,
    og_out, w_out,
    g, qv, kv, cw, pool, pool_t, mid, fine, kt, qt,
    c0r, s1, r1, s2, r2, s3, r3, d0s, d0r,
    eye, perm, mean1, mean2, mean3, up3, up2, up1,
    stage, colp, rowp, padt, win_t, wacc,
    a0r, xs, a1s, a1r, a2s, a2r, a3, a4, a0b, ogs,
    in_sem, send_sem, recv_sem,
):
    pb, ka = lax.axis_index("pb"), lax.axis_index("ka")
    core = pb % 2
    cy = (pb // 2) % 4
    zh = pb // 8
    cx = ka % 4
    zl = ka // 4
    cz = zh * 2 + zl

    def device(x, y, z, c):
        return {"pb": ((z // 2) * 4 + y) * 2 + c, "ka": (z % 2) * 4 + x}

    def shift(dim, d):
        return device(
            (cx + d) % 4 if dim == 0 else cx,
            (cy + d) % 4 if dim == 1 else cy,
            (cz + d) % 4 if dim == 2 else cz,
            core,
        )

    other_core = device(cx, cy, cz, 1 - core)
    pb_up = {"pb": (pb + 15) % 16, "ka": ka}
    pb_down = {"pb": (pb + 1) % 16, "ka": ka}
    ka_up = {"pb": pb, "ka": (ka + 7) % 8}
    ka_down = {"pb": pb, "ka": (ka + 1) % 8}

    loads = []
    used = [0]

    def group():
        used[0] += 1
        return used[0] - 1

    def send(src, dst, dev, k, n, whole):
        pltpu.make_async_remote_copy(
            src_ref=src, dst_ref=dst, send_sem=send_sem.at[k], recv_sem=recv_sem.at[n],
            device_id=dev, device_id_type=MESH,
        ).start()
        return whole, n

    def arrived(item):
        whole, n = item
        pltpu.make_async_copy(whole, whole, recv_sem.at[n]).wait()

    def load(src, dst):
        copy = pltpu.make_async_copy(src, dst, in_sem.at[len(loads)])
        copy.start()
        loads.append(copy)
        return copy

    ld_k = load(k_hbm, kv)
    ld_q = load(q_hbm, qv)
    ld_gc = load(g_hbm.at[pl.ds(3072, 1008)], g.at[pl.ds(3072, 1008)])
    ld_img = [load(qi_hbm, stage.at[0, pl.ds(0, 192)]), load(ki_hbm, stage.at[1, pl.ds(0, 192)])]
    ld_g = [load(g_hbm.at[pl.ds(768 * i, 768)], g.at[pl.ds(768 * i, 768)]) for i in range(4)]
    ld_cw = load(cw_hbm, cw)

    barrier = pltpu.get_barrier_semaphore()
    partners = [other_core, pb_up, pb_down, ka_up, ka_down]
    partners += [shift(dim, d) for dim in range(3) for d in (1, 2, 3)]
    for partner in partners:
        pl.semaphore_signal(barrier, inc=1, device_id=partner, device_id_type=MESH)

    for s in range(4):
        stage[s, 288:ST, :] = jnp.zeros((ST - 288, 256), BF)
    g[CELLS:4096, :] = jnp.zeros((4096 - CELLS, QN), BF)
    pool[CELLS:4096, :] = jnp.zeros((4096 - CELLS, 256), BF)

    rows_of = (8, 12, 8, 12)
    cols_of = (24, 16, 24, 16)

    def tile_index(s, i, j):
        return j * 12 + i if s == 3 else i * cols_of[s] + j

    @jax.named_scope("halo_cols")
    def halo_cols(s):
        n_r, n_c = rows_of[s], cols_of[s]
        v = col(32)
        i = v & 15
        src = jnp.where(v < 16, tile_index(s, i, 0), tile_index(s, i, n_c - 1))
        src = jnp.where(i < n_r, src, -1)
        colp[s] = dot(select(src, 192), stage[s, 0:192, :]).astype(BF)
        n = group()
        whole = stage.at[s, pl.ds(192, 32)]
        send(colp.at[s, pl.ds(0, 16)], stage.at[s, pl.ds(208, 16)], ka_up, 0, n, whole)
        return send(colp.at[s, pl.ds(16, 16)], stage.at[s, pl.ds(192, 16)], ka_down, 0, n, whole)

    @jax.named_scope("halo_rows")
    def halo_rows(s):
        n_r, n_c = rows_of[s], cols_of[s]
        v = col(64)
        j = (v & 31) - 1
        i = jnp.where(v < 32, 0, n_r - 1)
        src = tile_index(s, i, j)
        src = jnp.where(j < 0, jnp.where(ka == 0, -1, 192 + i), src)
        src = jnp.where(j == n_c, jnp.where(ka == 7, -1, 208 + i), src)
        src = jnp.where(j > n_c, -1, src)
        rowp[s] = dot(select(src, 224), stage[s, 0:224, :]).astype(BF)
        n = group()
        whole = stage.at[s, pl.ds(224, 64)]
        send(rowp.at[s, pl.ds(0, 32)], stage.at[s, pl.ds(256, 32)], pb_up, 1, n, whole)
        return send(rowp.at[s, pl.ds(32, 32)], stage.at[s, pl.ds(224, 32)], pb_down, 1, n, whole)

    def padded(s):
        n_r, n_c = rows_of[s], cols_of[s]
        v = col(QP)
        ip = div(v, n_c + 2)
        jp = v - ip * (n_c + 2)
        i, j = ip - 1, jp - 1
        src = tile_index(s, i, j)
        src = jnp.where(j < 0, jnp.where(ka == 0, -1, 192 + i), src)
        src = jnp.where(j == n_c, jnp.where(ka == 7, -1, 208 + i), src)
        src = jnp.where(i < 0, jnp.where(pb == 0, -1, 224 + jp), src)
        src = jnp.where(i == n_r, jnp.where(pb == 15, -1, 256 + jp), src)
        src = jnp.where(i > n_r, -1, src)
        return dot(select(src, ST), stage[s]).astype(BF)

    def tap_offset(s, rs, cs):
        pitch = cols_of[s] + 2
        return cs * pitch + rs if s % 2 else rs * pitch + cs

    flight = {}

    @jax.named_scope("tables")
    def tables():
        o = col(256)
        eye[...] = select(o, 256)
        perm[...] = select((o & 15) * 16 + lax.shift_right_logical(o, 4), 256)
        k = row(512)
        mean1[...] = pick(lax.shift_right_logical(k & 15, 1) * 16 + lax.shift_right_logical(k, 5), 128, 0.25)
        k = row(1024)
        mean2[...] = pick(lax.shift_right_logical(k & 15, 2) * 16 + lax.shift_right_logical(k, 6), 64, 0.0625)
        k = row(3072)
        key = (lax.shift_right_logical(k, 3) & 1) * 24 + lax.shift_right_logical(k, 7)
        mean3[...] = pick(key, 48, 0.015625)
        v = col(192)
        r = div(v, 48)
        up3[...] = select(lax.shift_right_logical(r, 1) * 24 + lax.shift_right_logical(v - r * 48, 1), 48)
        v = col(768)
        r = div(v, 96)
        up2[...] = select(lax.shift_right_logical(r, 1) * 48 + lax.shift_right_logical(v - r * 96, 1), 192)
        v = col(384)
        r = div(v, 192)
        up1[...] = select(lax.shift_right_logical(v - r * 192, 1), 96)

    @jax.named_scope("pool_keys")
    def pool_keys():
        for b in range(12):
            block = dot(perm[...], kv[256 * b:256 * b + 256, :]).astype(BF)
            for r in range(16):
                pool[192 * r + 16 * b:192 * r + 16 * b + 16, :] = block[16 * r:16 * r + 16, :]
        for b in range(6):
            block = dot(mean1[...], kv[512 * b:512 * b + 512, :]).astype(BF)
            for r in range(8):
                at = 3072 + 96 * r + 16 * b
                pool[at:at + 16, :] = block[16 * r:16 * r + 16, :]
        for b in range(3):
            block = dot(mean2[...], kv[1024 * b:1024 * b + 1024, :]).astype(BF)
            for r in range(4):
                at = 3840 + 48 * r + 16 * b
                pool[at:at + 16, :] = block[16 * r:16 * r + 16, :]
        pool[4032:4080, :] = dot(mean3[...], kv[...]).astype(BF)
        for b in range(16):
            pool_t[:, 256 * b:256 * b + 256] = dot_nt(eye[...], pool[256 * b:256 * b + 256, :]).astype(BF)

    @jax.named_scope("coarse_levels")
    def coarse_levels():
        l3 = (dot(g[4032:4080, :], qv[...]) * (1.0 / 64.0)).astype(BF)
        l2 = (dot(g[3840:4032, :], qv[...]) * (1.0 / 16.0) + dot(up3[...], l3)).astype(BF)
        mid[...] = (dot(g[3072:3840, :], qv[...]) * 0.25 + dot(up2[...], l2)).astype(BF)

    @jax.named_scope("key_rows")
    def key_rows(h):
        fine[h % 2] = dot(g[384 * h:384 * h + 384, :], qv[...]) + dot(up1[...], mid[96 * h:96 * h + 96, :])

    def key_tiles(h):
        for t in range(8):
            for p in range(2):
                for r in range(2):
                    at, to = 192 * r + 24 * t + 12 * p, 24 * (h % 2) + 12 * r
                    kt[h // 2, p, t, to:to + 12, :] = fine[h % 2, at:at + 12, :]

    def core_send(i):
        flight[i, 0] = send(kt.at[i, 1 - core], c0r.at[i], other_core, 2, group(), c0r.at[i])

    @jax.named_scope("query_chunk")
    def query_chunk(i):
        part = dot(pool_t[...], g[:, 384 * i:384 * i + 384])
        part = jnp.transpose(part)
        for hh in range(2):
            for k in range(8):
                at = 192 * hh + 24 * k
                qt[i, k, 24 * hh:24 * hh + 24, :] = part[at:at + 24, :]

    def along(u):
        return (1, cy, zh) if u < 4 else (0, cx, zl)

    def part_of(u, g_, n, c):
        lanes = slice(128 * c, 128 * c + 128)
        tile = g_ * 4 + n
        if u < 4:
            return kt[u, core, tile, :, lanes]
        return qt[u - 4, tile, :, lanes]

    def mates(u):
        dim, n, _ = along(u)
        flip = n + 1 - 2 * (n % 2)
        mirror = 3 - n
        return ((flip, mirror), (mirror, flip))

    def ring(u, n):
        dim = along(u)[0]
        return device(n if dim == 0 else cx, n if dim == 1 else cy, cz, core)

    def last_mate(u):
        if u < 4:
            return device(cx, cy, (1 - zh) * 2 + zl, core)
        return device(cx, cy, zh * 2 + (1 - zl), core)

    @jax.named_scope("step1")
    def step1(u):
        sem = group()
        for c in range(2):
            first, _ = mates(u)[c]
            flip = first + 1 - 2 * (first % 2)
            beyond = (3 - first) if c == 0 else flip
            for j in range(4):
                n = first if j < 2 else beyond
                s1[u, c, j] = part_of(u, j % 2, n, c).astype(BF)
            flight[u, 1] = send(s1.at[u, c], r1.at[u, c], ring(u, first), 3, sem, r1.at[u])

    @jax.named_scope("step2")
    def step2(u):
        sem = group()
        arrived(flight[u, 1])
        for c in range(2):
            _, second = mates(u)[c]
            for j in range(2):
                s2[u, c, j] = (part_of(u, j, second, c) + r1[u, c, 2 + j].astype(F32)).astype(BF)
            flight[u, 2] = send(s2.at[u, c], r2.at[u, c], ring(u, second), 4, sem, r2.at[u])

    @jax.named_scope("step3")
    def step3(u):
        sem = group()
        _, n, z = along(u)
        arrived(flight[u, 2])
        for c in range(2):
            far = part_of(u, 1 - z, n, c) + r1[u, c, 1 - z].astype(F32) + r2[u, c, 1 - z].astype(F32)
            s3[u, c] = far.astype(BF)
            flight[u, 3] = send(s3.at[u, c], r3.at[u, c], last_mate(u), 5, sem, r3.at[u])

    @jax.named_scope("finish")
    def finish(u):
        _, n, z = along(u)
        s = 3 if u < 4 else 2
        at = 48 * (u % 4)
        arrived(flight[u, 3])
        for c in range(2):
            total = part_of(u, z, n, c) + r1[u, c, z].astype(F32) + r2[u, c, z].astype(F32)
            total = (total + r3[u, c].astype(F32)) * 0.0625
            stage[s, at:at + 48, 128 * c:128 * c + 128] = total.astype(BF)

    @jax.named_scope("direct")
    def direct():
        n = group()
        for k in range(8):
            d0s[k] = qt[3, k].astype(BF)
        for dz in range(2):
            for dx in range(4):
                if dz + dx:
                    z, x = (zl + dz) % 2, (cx + dx) % 4
                    flight[7, 1] = send(
                        d0s.at[z * 4 + x], d0r.at[dz * 4 + dx - 1], device(x, cy, zh * 2 + z, core), 13, n, d0r
                    )

    @jax.named_scope("direct_finish")
    def direct_finish():
        arrived(flight[7, 1])
        total = qt[3, zl * 4 + cx]
        for k in range(7):
            total = total + d0r[k].astype(F32)
        stage[2, 144:192, :] = (total * 0.0625).astype(BF)

    @jax.named_scope("core_step")
    def core_step(u):
        arrived(flight[u, 0])
        kt[u, core] = kt[u, core] + c0r[u]
        step1(u)

    @jax.named_scope("image_windows")
    def image_windows(s):
        padt[s] = dot_nt(eye[...], padded(s)).astype(BF)
        v = col(192)
        if s == 0:
            i = div(v, 24)
            f = i * 26 + (v - i * 24)
        else:
            j = div(v, 12)
            f = (v - j * 12) * 18 + j
        for rs in range(3):
            for cs in range(3):
                sel = select(f + tap_offset(s, rs, cs), QP)
                win_t[s, rs * 3 + cs] = dot_nt(padt[s], sel).astype(BF)

    @jax.named_scope("weight_part")
    def weight_part(s, first):
        for t in range(9):
            term = dot(win_t[s, t], stage[s + 2, 0:192, :])
            j, k = t // 3, t % 3
            for h in range(2):
                half = term[:, 128 * h:128 * h + 128]
                rows = slice(256 * k, 256 * k + 256)
                wacc[h, j, rows] = half if first else wacc[h, j, rows] + half
            if not first and k == 2:
                f0.append(send(wacc.at[1 - core, j], a0r.at[j], other_core, 6, group(), a0r.at[j]))

    @jax.named_scope("input_grad")
    def input_grad(s, slot):
        pad = padded(s)
        v = col(192)
        if s == 2:
            i = div(v, 24)
            f = i * 26 + (v - i * 24)
        else:
            f = lax.shift_right_logical(v, 4) * 18 + (v & 15)
        acc = jnp.zeros((192, 256), F32)
        for rs in range(3):
            for cs in range(3):
                sel = select(f + tap_offset(s, 2 - rs, 2 - cs), QP)
                win = dot(sel, pad).astype(BF)
                at = 256 * (rs * 3 + cs)
                acc = acc + dot_nt(win, cw[at:at + 256, :])
        ogs[slot] = acc.astype(BF)

    f0 = []
    tables()
    ld_k.wait()
    pool_keys()
    ld_q.wait()
    ld_gc.wait()
    coarse_levels()
    ld_g[0].wait()
    key_rows(0)
    key_rows(1)
    key_tiles(0)
    ld_g[1].wait()
    key_rows(2)
    key_tiles(1)
    for c in ld_img:
        c.wait()
    pl.semaphore_wait(barrier, len(partners))
    core_send(0)
    hc = [halo_cols(0), halo_cols(1)]
    key_rows(3)
    key_tiles(2)
    ld_g[2].wait()
    key_rows(4)
    key_tiles(3)
    core_send(1)
    core_step(0)
    key_rows(5)
    key_tiles(4)
    ld_g[3].wait()
    key_rows(6)
    key_tiles(5)
    core_send(2)
    core_step(1)

    def queries(i):
        query_chunk(i)
        step1(4 + i)

    queries(0)
    core_step(2)
    step2(0)
    key_rows(7)
    key_tiles(6)
    key_tiles(7)
    core_send(3)
    hr = []
    for s in range(2):
        arrived(hc[s])
        hr.append(halo_rows(s))
    queries(1)
    step2(1)
    core_step(3)
    step3(0)
    queries(2)
    step2(2)
    step2(4)
    query_chunk(3)
    direct()
    step2(5)
    step2(3)
    step3(1)
    step3(2)
    step3(4)
    arrived(hr[1])
    image_windows(1)
    step2(6)
    step3(3)
    step3(5)
    arrived(hr[0])
    image_windows(0)
    step3(6)
    for u in range(4):
        finish(u)
    hk = halo_cols(3)
    weight_part(1, True)
    for u in range(4, 7):
        finish(u)
    direct_finish()
    hq = halo_cols(2)
    weight_part(0, False)

    coords = (cx, cy, cz)
    f1 = []
    for j in range(3):
        arrived(f0[j])
        n = coords[j]
        wacc[core, j] = wacc[core, j] + a0r[j]
        for k in range(4):
            a1s[j, k] = wacc[core, j, 192 * k:192 * k + 192].astype(BF)
        sem = group()
        for d in (1, 2, 3):
            last = send(a1s.at[j, (n + d) % 4], a1r.at[j, d - 1], shift(j, d), 7, sem, a1r.at[j])
        f1.append(last)
    arrived(hk)
    hk = halo_rows(3)
    ld_cw.wait()
    f2 = []
    for j in range(3):
        arrived(f1[j])
        x = wacc[core, j, pl.ds(pl.multiple_of(192 * coords[j], 192), 192), :]
        for d in range(3):
            x = x + a1r[j, d].astype(F32)
        xs[j] = x
        for n in range(4):
            a2s[j, n] = x[48 * n:48 * n + 48, :].astype(BF)
        b = (j + 1) % 3
        sem = group()
        for d in (1, 2, 3):
            last = send(a2s.at[j, (coords[b] + d) % 4], a2r.at[j, d - 1], shift(b, d), 8, sem, a2r.at[j])
        f2.append(last)
    arrived(hq)
    hq = halo_rows(2)
    arrived(hk)
    input_grad(3, 1)
    f3 = []
    for j in range(3):
        arrived(f2[j])
        b, e = (j + 1) % 3, (j + 2) % 3
        y = xs[j, pl.ds(pl.multiple_of(coords[b] * 48, 48), 48), :]
        for d in range(3):
            y = y + a2r[j, d].astype(F32)
        a3[j, 0] = y.astype(BF)
        sem = group()
        for d in (1, 2, 3):
            last = send(a3.at[j, 0], a3.at[j, d], shift(e, d), 9, sem, a3.at[j, pl.ds(1, 3)])
        f3.append(last)
    arrived(hq)
    input_grad(2, 0)
    copies = [load(ogs, og_out)]
    f4 = []
    own = []
    for j in range(3):
        arrived(f3[j])
        b, e = (j + 1) % 3, (j + 2) % 3
        y = jnp.zeros((48, 128), F32)
        for k in range(4):
            y = y + a3[j, (coords[e] + 4 - k) % 4].astype(F32)
        a4[j] = y.astype(BF)
        mine = w_out.at[core, j, coords[j], coords[b]]
        sem = group()
        for d in (1, 2, 3):
            last = send(a4.at[j], mine, shift(b, d), 10, sem, a2r.at[j])
        own.append(load(a4.at[j], mine))
        f4.append(last)
    f5 = []
    for j in range(3):
        arrived(f4[j])
        own[j].wait()
        mine = w_out.at[core, j, coords[j]]
        sem = group()
        for d in (1, 2, 3):
            last = send(mine, mine, shift(j, d), 11, sem, a1r.at[j])
        f5.append(last)
    f6 = []
    for j in range(3):
        arrived(f5[j])
        mine = w_out.at[core, j]
        f6.append(send(mine, mine, other_core, 12, group(), mine))
    for j in range(3):
        arrived(f6[j])
    sent = (colp, rowp, c0r, s1, s2, s3, a0r, a1r, a2r, a2r, a2r, a1r, a0b, d0r)
    for k, ref in enumerate(sent):
        pltpu.make_async_copy(ref, ref, send_sem.at[k]).wait()
    copies[0].wait()


def widen(og, w, qg_out, kg_out, w_out, wide, sem):
    copies = [
        pltpu.make_async_copy(og.at[0], qg_out, sem.at[0]),
        pltpu.make_async_copy(og.at[1], kg_out, sem.at[1]),
    ]
    for k in range(6):
        rows = pl.ds(384 * k, 384)
        for h in range(2):
            wide[384 * k:384 * k + 384, 128 * h:128 * h + 128] = w[h, 384 * k:384 * k + 384, :].astype(F32)
        copies.append(pltpu.make_async_copy(wide.at[rows], w_out.at[rows], sem.at[2 + k]))
        if k == 0:
            copies[0].start()
            copies[1].start()
        copies[-1].start()
    for c in copies:
        c.wait()


def vmem(*shape, dtype=BF):
    return pltpu.VMEM(shape, dtype)


def body(query_features, key_features, pyramid_grad, query_image, key_image, conv_weight):
    cells = jnp.transpose(pyramid_grad.reshape(QN, CELLS))
    anywhere = pl.BlockSpec(memory_space=pl.ANY)
    og, w = pl.pallas_call(
        kernel,
        out_shape=(
            jax.ShapeDtypeStruct((2, 192, 256), BF),
            jax.ShapeDtypeStruct((2, 3, 4, 4, 48, 128), BF),
        ),
        in_specs=[pl.BlockSpec(memory_space=pltpu.HBM)] * 6,
        out_specs=[pl.BlockSpec(memory_space=pl.ANY)] * 2,
        scratch_shapes=[
            vmem(4096, QN), vmem(QN, 256), vmem(3072, 256), vmem(2304, 256),
            vmem(4096, 256), vmem(256, 4096), vmem(768, 256), vmem(2, 384, 256, dtype=F32),
            vmem(4, 2, 8, 48, 256, dtype=F32), vmem(4, 8, 48, 256, dtype=F32),
            vmem(4, 8, 48, 256, dtype=F32),
            vmem(7, 2, 4, 48, 128), vmem(7, 2, 4, 48, 128),
            vmem(7, 2, 2, 48, 128), vmem(7, 2, 2, 48, 128),
            vmem(7, 2, 48, 128), vmem(7, 2, 48, 128),
            vmem(8, 48, 256), vmem(7, 48, 256),
            vmem(256, 256), vmem(256, 256), vmem(128, 512), vmem(64, 1024), vmem(48, 3072),
            vmem(192, 48), vmem(768, 192), vmem(384, 96),
            vmem(4, ST, 256), vmem(4, 32, 256), vmem(4, 64, 256),
            vmem(2, 256, QP), vmem(2, 9, 256, 192), vmem(2, 3, 768, 128, dtype=F32),
            vmem(3, 768, 128, dtype=F32), vmem(3, 192, 128, dtype=F32),
            vmem(3, 4, 192, 128), vmem(3, 3, 192, 128),
            vmem(3, 4, 48, 128), vmem(3, 3, 48, 128), vmem(3, 4, 48, 128),
            vmem(3, 48, 128), vmem(3, 4, 4, 48, 128), vmem(2, 192, 256),
            pltpu.SemaphoreType.DMA((14,)),
            pltpu.SemaphoreType.DMA((14,)),
            pltpu.SemaphoreType.DMA((55,)),
        ],
        compiler_params=pltpu.CompilerParams(
            collective_id=0, has_side_effects=True, vmem_limit_bytes=VMEM_BYTES
        ),
    )(
        *[
            pltpu.with_memory_space_constraint(x, pltpu.HBM)
            for x in (
                cells,
                query_features.reshape(QN, 256),
                key_features.reshape(3072, 256),
                query_image.reshape(192, 256),
                key_image.reshape(192, 256),
                conv_weight.reshape(2304, 256),
            )
        ]
    )
    qg, kg, w = pl.pallas_call(
        widen,
        out_shape=(
            jax.ShapeDtypeStruct((192, 256), BF),
            jax.ShapeDtypeStruct((192, 256), BF),
            jax.ShapeDtypeStruct((2304, 256), F32),
        ),
        in_specs=[pl.BlockSpec(memory_space=pltpu.VMEM)] * 2,
        out_specs=[pl.BlockSpec(memory_space=pltpu.HBM)] * 3,
        scratch_shapes=[vmem(2304, 256, dtype=F32), pltpu.SemaphoreType.DMA((8,))],
        compiler_params=pltpu.CompilerParams(vmem_limit_bytes=16 * 1024 * 1024),
    )(og, w.reshape(2, 2304, 128))
    return qg.reshape(8, 24, 256), kg.reshape(12, 16, 256), w.reshape(3, 3, 256, 256)


def solution(mesh):
    placed = (
        P("pb", None, None),
        P(None, "ka", None),
        P("pb", "ka", None),
        P("pb", "ka", None),
        P("pb", "ka", None),
        P(),
    )
    return jax.shard_map(
        body,
        mesh=mesh,
        in_specs=placed,
        out_specs=(P("pb", "ka", None), P("pb", "ka", None), P()),
        check_vma=False,
    )
```

time: 78.9 us -> 63.6 us (0.81)
  local copies, waits for them, and re-layouts: 13.1 us -> 0 us
  other arithmetic: 1.42 us -> 0 us
  Pallas kernels: 63.5 us -> 62.7 us
    convert_element_type x2 -> x0, local copies, waits for them, and re-layouts: 11.8 us -> none  [body(): return (qg.reshape(8, 24, 256), kg.reshape(12, 16, 256), w.astype(F32))]
    convert_element_type x1 -> x0, other arithmetic: 1.42 us -> none  [body(): return (qg.reshape(8, 24, 256), kg.reshape(12, 16, 256), w.astype(F32))]
    unnamed x6 -> x0, local copies, waits for them, and re-layouts: 1.29 us -> none
    pallas_call x1 -> x2, Pallas kernels: 63.5 us -> 62.7 us  [the longest x1 61.2 us: body(): pl.pallas_call(kernel, out_shape=(jax.ShapeDtypeStruct((2, 192, 256), BF)...]
where the time goes in v2:
time: 63.6 us; the launch traced here: 63.5 us
  Pallas kernels  62.7 us (99%)
  between operations  0.8 us (1%)
    pallas_call x1, Pallas kernels, body(): pl.pallas_call(kernel, out_shape=(jax.ShapeDtypeStruct((2, 192, 256), BF)...  61.2 us
    pallas_call x1, Pallas kernels, body(): pl.pallas_call(widen, out_shape=(jax.ShapeDtypeStruct((192, 256), BF), ja...  1.53 us

profile of v2, /device:TPU:1, one launch (start us, length us, event | category | flops | bytes accessed | tf_op | source)
XLA Modules:
  0.0 63.5 jit_solution(9978939234850151281)
XLA Ops:
  0.6 61.2 %shard_map.85 = (bf16[2,192,256]{2,1,0:T(8,128)(2,1)S(1)}, bf16[2,3,4,4,48,128]{5,4,3,2,1,0:T(8,128)(2,1)S(1)}) custom-call(bf16[4080,1536]{1,0:T(8,128)(2,1)} %bitcast.13, bf16[1536,256]{1,0:T(8,128)(2,1)} %bitcast.16, bf16[3072,256]{1,0:T(8,128)(2,1)} %bitcast.14, bf16[192,256]{1,0:T(8,128)(2,1)} %bitcast.17, bf16[192,256]{1,0:T(8,128)(2,1)} %bitcast.18, ...), custom_call_target="tpu_custom_call" | custom-call | tf_op jit(solution)/shard_map/pallas_call | solution.py:583
  61.8 1.5 %shard_map.86 = (bf16[192,256]{1,0:T(8,128)(2,1)}, bf16[192,256]{1,0:T(8,128)(2,1)}, f32[2304,256]{1,0:T(8,128)}) custom-call(bf16[2,192,256]{2,1,0:T(8,128)(2,1)S(1)} %get-tuple-element.8.og, bf16[2,2304,128]{2,1,0:T(8,128)(2,1)S(1)} %bitcast.12), custom_call_target="tpu_custom_call" | custom-call | tf_op jit(solution)/shard_map/pallas_call | solution.py:628

commit v3 on v2

--- a/solution.py
+++ b/solution.py
@@ -53,7 +53,7 @@
     c0r, s1, r1, s2, r2, s3, r3, d0s, d0r,
     eye, perm, mean1, mean2, mean3, up3, up2, up1,
     stage, colp, rowp, padt, win_t, wacc,
-    a0r, xs, a1s, a1r, a2s, a2r, a3, a4, a0b, ogs,
+    a0r, a1s, a1r, a2, a3, a4, ogs,
     in_sem, send_sem, recv_sem,
 ):
     pb, ka = lax.axis_index("pb"), lax.axis_index("ka")
@@ -228,7 +228,8 @@
 
     @jax.named_scope("key_rows")
     def key_rows(h):
-        fine[h % 2] = dot(g[384 * h:384 * h + 384, :], qv[...]) + dot(up1[...], mid[96 * h:96 * h + 96, :])
+        left = jnp.concatenate([g[384 * h:384 * h + 384, :], up1[...]], axis=1)
+        fine[h % 2] = dot(left, jnp.concatenate([qv[...], mid[96 * h:96 * h + 96, :]], axis=0))
 
     def key_tiles(h):
         for t in range(8):
@@ -327,7 +328,7 @@
                 if dz + dx:
                     z, x = (zl + dz) % 2, (cx + dx) % 4
                     flight[7, 1] = send(
-                        d0s.at[z * 4 + x], d0r.at[dz * 4 + dx - 1], device(x, cy, zh * 2 + z, core), 13, n, d0r
+                        d0s.at[z * 4 + x], d0r.at[dz * 4 + dx - 1], device(x, cy, zh * 2 + z, core), 12, n, d0r
                     )
 
     @jax.named_scope("direct_finish")
@@ -450,15 +451,15 @@
     step2(5)
     step2(3)
     step3(1)
-    step3(2)
-    step3(4)
     arrived(hr[1])
     image_windows(1)
     step2(6)
+    step3(2)
+    step3(4)
+    arrived(hr[0])
+    image_windows(0)
     step3(3)
     step3(5)
-    arrived(hr[0])
-    image_windows(0)
     step3(6)
     for u in range(4):
         finish(u)
@@ -491,65 +492,53 @@
         x = wacc[core, j, pl.ds(pl.multiple_of(192 * coords[j], 192), 192), :]
         for d in range(3):
             x = x + a1r[j, d].astype(F32)
-        xs[j] = x
-        for n in range(4):
-            a2s[j, n] = x[48 * n:48 * n + 48, :].astype(BF)
-        b = (j + 1) % 3
+        a2[j, 0] = x.astype(BF)
         sem = group()
         for d in (1, 2, 3):
-            last = send(a2s.at[j, (coords[b] + d) % 4], a2r.at[j, d - 1], shift(b, d), 8, sem, a2r.at[j])
+            last = send(a2.at[j, 0], a2.at[j, d], shift((j + 1) % 3, d), 8, sem, a2.at[j, pl.ds(1, 3)])
         f2.append(last)
     arrived(hq)
     hq = halo_rows(2)
     arrived(hk)
     input_grad(3, 1)
+
+    def ring_sum(ref, n):
+        y = ref[n].astype(F32)
+        for k in (1, 2, 3):
+            y = y + ref[(n + 4 - k) % 4].astype(F32)
+        return y.astype(BF)
+
     f3 = []
     for j in range(3):
         arrived(f2[j])
-        b, e = (j + 1) % 3, (j + 2) % 3
-        y = xs[j, pl.ds(pl.multiple_of(coords[b] * 48, 48), 48), :]
-        for d in range(3):
-            y = y + a2r[j, d].astype(F32)
-        a3[j, 0] = y.astype(BF)
+        a3[j, 0] = ring_sum(a2.at[j], coords[(j + 1) % 3])
         sem = group()
         for d in (1, 2, 3):
-            last = send(a3.at[j, 0], a3.at[j, d], shift(e, d), 9, sem, a3.at[j, pl.ds(1, 3)])
+            last = send(a3.at[j, 0], a3.at[j, d], shift((j + 2) % 3, d), 9, sem, a3.at[j, pl.ds(1, 3)])
         f3.append(last)
     arrived(hq)
     input_grad(2, 0)
     copies = [load(ogs, og_out)]
-    f4 = []
+    f5 = []
     own = []
     for j in range(3):
         arrived(f3[j])
-        b, e = (j + 1) % 3, (j + 2) % 3
-        y = jnp.zeros((48, 128), F32)
-        for k in range(4):
-            y = y + a3[j, (coords[e] + 4 - k) % 4].astype(F32)
-        a4[j] = y.astype(BF)
-        mine = w_out.at[core, j, coords[j], coords[b]]
-        sem = group()
-        for d in (1, 2, 3):
-            last = send(a4.at[j], mine, shift(b, d), 10, sem, a2r.at[j])
-        own.append(load(a4.at[j], mine))
-        f4.append(last)
-    f5 = []
-    for j in range(3):
-        arrived(f4[j])
-        own[j].wait()
+        a4[j] = ring_sum(a3.at[j], coords[(j + 2) % 3])
         mine = w_out.at[core, j, coords[j]]
         sem = group()
         for d in (1, 2, 3):
-            last = send(mine, mine, shift(j, d), 11, sem, a1r.at[j])
+            last = send(a4.at[j], mine, shift(j, d), 10, sem, a1r.at[j])
         f5.append(last)
+        own.append(load(a4.at[j], mine))
     f6 = []
     for j in range(3):
         arrived(f5[j])
+        own[j].wait()
         mine = w_out.at[core, j]
-        f6.append(send(mine, mine, other_core, 12, group(), mine))
+        f6.append(send(mine, mine, other_core, 11, group(), mine))
     for j in range(3):
         arrived(f6[j])
-    sent = (colp, rowp, c0r, s1, s2, s3, a0r, a1r, a2r, a2r, a2r, a1r, a0b, d0r)
+    sent = (colp, rowp, c0r, s1, s2, s3, a0r, a1r, a1r, a1r, a1r, a1s, d0r)
     for k, ref in enumerate(sent):
         pltpu.make_async_copy(ref, ref, send_sem.at[k]).wait()
     copies[0].wait()
@@ -584,7 +573,7 @@
         kernel,
         out_shape=(
             jax.ShapeDtypeStruct((2, 192, 256), BF),
-            jax.ShapeDtypeStruct((2, 3, 4, 4, 48, 128), BF),
+            jax.ShapeDtypeStruct((2, 3, 4, 192, 128), BF),
         ),
         in_specs=[pl.BlockSpec(memory_space=pltpu.HBM)] * 6,
         out_specs=[pl.BlockSpec(memory_space=pl.ANY)] * 2,
@@ -601,13 +590,12 @@
             vmem(192, 48), vmem(768, 192), vmem(384, 96),
             vmem(4, ST, 256), vmem(4, 32, 256), vmem(4, 64, 256),
             vmem(2, 256, QP), vmem(2, 9, 256, 192), vmem(2, 3, 768, 128, dtype=F32),
-            vmem(3, 768, 128, dtype=F32), vmem(3, 192, 128, dtype=F32),
+            vmem(3, 768, 128, dtype=F32),
             vmem(3, 4, 192, 128), vmem(3, 3, 192, 128),
-            vmem(3, 4, 48, 128), vmem(3, 3, 48, 128), vmem(3, 4, 48, 128),
-            vmem(3, 48, 128), vmem(3, 4, 4, 48, 128), vmem(2, 192, 256),
+            vmem(3, 4, 192, 128), vmem(3, 4, 192, 128), vmem(3, 192, 128), vmem(2, 192, 256),
             pltpu.SemaphoreType.DMA((14,)),
-            pltpu.SemaphoreType.DMA((14,)),
-            pltpu.SemaphoreType.DMA((55,)),
+            pltpu.SemaphoreType.DMA((13,)),
+            pltpu.SemaphoreType.DMA((52,)),
         ],
         compiler_params=pltpu.CompilerParams(
             collective_id=0, has_side_effects=True, vmem_limit_bytes=VMEM_BYTES

time: 63.6 us -> 60.8 us (0.956)
  Pallas kernels: 62.7 us -> 59.9 us
    pallas_call x1, Pallas kernels: 61.2 us -> 58.4 us  [body(): pl.pallas_call(kernel, out_shape=(jax.ShapeDtypeStruct((2, 192, 256), BF)...]
where the time goes in v3:
time: 60.8 us; the launch traced here: 60.7 us
  Pallas kernels  59.9 us (99%)
  between operations  0.8 us (1%)
    pallas_call x1, Pallas kernels, body(): pl.pallas_call(kernel, out_shape=(jax.ShapeDtypeStruct((2, 192, 256), BF)...  58.4 us
    pallas_call x1, Pallas kernels, body(): pl.pallas_call(widen, out_shape=(jax.ShapeDtypeStruct((192, 256), BF), ja...  1.53 us

profile of v3, /device:TPU:1, one launch (start us, length us, event | category | flops | bytes accessed | tf_op | source)
XLA Modules:
  0.0 60.7 jit_solution(17855870261402536051)
XLA Ops:
  0.6 58.4 %shard_map.85 = (bf16[2,192,256]{2,1,0:T(8,128)(2,1)S(1)}, bf16[2,3,4,192,128]{4,3,2,1,0:T(8,128)(2,1)S(1)}) custom-call(bf16[4080,1536]{1,0:T(8,128)(2,1)} %bitcast.13, bf16[1536,256]{1,0:T(8,128)(2,1)} %bitcast.16, bf16[3072,256]{1,0:T(8,128)(2,1)} %bitcast.14, bf16[192,256]{1,0:T(8,128)(2,1)} %bitcast.17, bf16[192,256]{1,0:T(8,128)(2,1)} %bitcast.18, ...), custom_call_target="tpu_custom_call" | custom-call | tf_op jit(solution)/shard_map/pallas_call | solution.py:572
  59.0 1.5 %shard_map.86 = (bf16[192,256]{1,0:T(8,128)(2,1)}, bf16[192,256]{1,0:T(8,128)(2,1)}, f32[2304,256]{1,0:T(8,128)}) custom-call(bf16[2,192,256]{2,1,0:T(8,128)(2,1)S(1)} %get-tuple-element.8.og, bf16[2,2304,128]{2,1,0:T(8,128)(2,1)S(1)} %bitcast.12), custom_call_target="tpu_custom_call" | custom-call | tf_op jit(solution)/shard_map/pallas_call | solution.py:616

commit v4 on v3

--- a/solution.py
+++ b/solution.py
@@ -105,7 +105,7 @@
         loads.append(copy)
         return copy
 
-    ld_k = load(k_hbm, kv)
+    ld_k = [load(k_hbm.at[pl.ds(1024 * i, 1024)], kv.at[pl.ds(1024 * i, 1024)]) for i in range(3)]
     ld_q = load(q_hbm, qv)
     ld_gc = load(g_hbm.at[pl.ds(3072, 1008)], g.at[pl.ds(3072, 1008)])
     ld_img = [load(qi_hbm, stage.at[0, pl.ds(0, 192)]), load(ki_hbm, stage.at[1, pl.ds(0, 192)])]
@@ -196,13 +196,14 @@
         v = col(768)
         r = div(v, 96)
         up2[...] = select(lax.shift_right_logical(r, 1) * 48 + lax.shift_right_logical(v - r * 96, 1), 192)
-        v = col(384)
         r = div(v, 192)
-        up1[...] = select(lax.shift_right_logical(v - r * 192, 1), 96)
+        up1[...] = select(lax.shift_right_logical(r, 1) * 96 + lax.shift_right_logical(v - r * 192, 1), 192)
 
     @jax.named_scope("pool_keys")
     def pool_keys():
         for b in range(12):
+            if b % 4 == 0:
+                ld_k[b // 4].wait()
             block = dot(perm[...], kv[256 * b:256 * b + 256, :]).astype(BF)
             for r in range(16):
                 pool[192 * r + 16 * b:192 * r + 16 * b + 16, :] = block[16 * r:16 * r + 16, :]
@@ -224,19 +225,25 @@
     def coarse_levels():
         l3 = (dot(g[4032:4080, :], qv[...]) * (1.0 / 64.0)).astype(BF)
         l2 = (dot(g[3840:4032, :], qv[...]) * (1.0 / 16.0) + dot(up3[...], l3)).astype(BF)
-        mid[...] = (dot(g[3072:3840, :], qv[...]) * 0.25 + dot(up2[...], l2)).astype(BF)
+        for k in range(3):
+            at = 256 * k
+            part = dot(g[3072 + at:3328 + at, :], qv[...]) * 0.25 + dot(up2[at:at + 256, :], l2)
+            mid[at:at + 256, :] = part.astype(BF)
 
     @jax.named_scope("key_rows")
-    def key_rows(h):
-        left = jnp.concatenate([g[384 * h:384 * h + 384, :], up1[...]], axis=1)
-        fine[h % 2] = dot(left, jnp.concatenate([qv[...], mid[96 * h:96 * h + 96, :]], axis=0))
-
-    def key_tiles(h):
+    def key_rows(i):
+        right = jnp.concatenate([qv[...], mid[192 * i:192 * i + 192, :]], axis=0)
+        for k in range(3):
+            at = 768 * i + 256 * k
+            left = jnp.concatenate([g[at:at + 256, :], up1[256 * k:256 * k + 256, :]], axis=1)
+            fine[i % 2, 256 * k:256 * k + 256, :] = dot(left, right)
+
+    def key_tiles(i):
         for t in range(8):
             for p in range(2):
-                for r in range(2):
-                    at, to = 192 * r + 24 * t + 12 * p, 24 * (h % 2) + 12 * r
-                    kt[h // 2, p, t, to:to + 12, :] = fine[h % 2, at:at + 12, :]
+                for r in range(4):
+                    at = 192 * r + 24 * t + 12 * p
+                    kt[i, p, t, 12 * r:12 * r + 12, :] = fine[i % 2, at:at + 12, :]
 
     def core_send(i):
         flight[i, 0] = send(kt.at[i, 1 - core], c0r.at[i], other_core, 2, group(), c0r.at[i])
@@ -392,37 +399,31 @@
 
     f0 = []
     tables()
-    ld_k.wait()
     pool_keys()
     ld_q.wait()
     ld_gc.wait()
     coarse_levels()
     ld_g[0].wait()
     key_rows(0)
-    key_rows(1)
     key_tiles(0)
-    ld_g[1].wait()
-    key_rows(2)
-    key_tiles(1)
     for c in ld_img:
         c.wait()
     pl.semaphore_wait(barrier, len(partners))
     core_send(0)
     hc = [halo_cols(0), halo_cols(1)]
-    key_rows(3)
-    key_tiles(2)
-    ld_g[2].wait()
-    key_rows(4)
-    key_tiles(3)
-    core_send(1)
+
+    def keys(i):
+        if i < 3:
+            ld_g[i].wait()
+        key_rows(i)
+        key_tiles(i)
+        core_send(i)
+
+    keys(1)
     core_step(0)
-    key_rows(5)
-    key_tiles(4)
+    keys(2)
+    core_step(1)
     ld_g[3].wait()
-    key_rows(6)
-    key_tiles(5)
-    core_send(2)
-    core_step(1)
 
     def queries(i):
         query_chunk(i)
@@ -431,10 +432,7 @@
     queries(0)
     core_step(2)
     step2(0)
-    key_rows(7)
-    key_tiles(6)
-    key_tiles(7)
-    core_send(3)
+    keys(3)
     hr = []
     for s in range(2):
         arrived(hc[s])
@@ -442,8 +440,8 @@
     queries(1)
     step2(1)
     core_step(3)
+    queries(2)
     step3(0)
-    queries(2)
     step2(2)
     step2(4)
     query_chunk(3)
@@ -579,7 +577,7 @@
         out_specs=[pl.BlockSpec(memory_space=pl.ANY)] * 2,
         scratch_shapes=[
             vmem(4096, QN), vmem(QN, 256), vmem(3072, 256), vmem(2304, 256),
-            vmem(4096, 256), vmem(256, 4096), vmem(768, 256), vmem(2, 384, 256, dtype=F32),
+            vmem(4096, 256), vmem(256, 4096), vmem(768, 256), vmem(2, 768, 256, dtype=F32),
             vmem(4, 2, 8, 48, 256, dtype=F32), vmem(4, 8, 48, 256, dtype=F32),
             vmem(4, 8, 48, 256, dtype=F32),
             vmem(7, 2, 4, 48, 128), vmem(7, 2, 4, 48, 128),
@@ -587,13 +585,13 @@
             vmem(7, 2, 48, 128), vmem(7, 2, 48, 128),
             vmem(8, 48, 256), vmem(7, 48, 256),
             vmem(256, 256), vmem(256, 256), vmem(128, 512), vmem(64, 1024), vmem(48, 3072),
-            vmem(192, 48), vmem(768, 192), vmem(384, 96),
+            vmem(192, 48), vmem(768, 192), vmem(768, 192),
             vmem(4, ST, 256), vmem(4, 32, 256), vmem(4, 64, 256),
             vmem(2, 256, QP), vmem(2, 9, 256, 192), vmem(2, 3, 768, 128, dtype=F32),
             vmem(3, 768, 128, dtype=F32),
             vmem(3, 4, 192, 128), vmem(3, 3, 192, 128),
             vmem(3, 4, 192, 128), vmem(3, 4, 192, 128), vmem(3, 192, 128), vmem(2, 192, 256),
-            pltpu.SemaphoreType.DMA((14,)),
+            pltpu.SemaphoreType.DMA((16,)),
             pltpu.SemaphoreType.DMA((13,)),
             pltpu.SemaphoreType.DMA((52,)),
         ],

time: 60.8 us -> 57.3 us (0.942)
  Pallas kernels: 59.9 us -> 56.4 us
    pallas_call x1, Pallas kernels: 58.4 us -> 54.9 us  [body(): pl.pallas_call(kernel, out_shape=(jax.ShapeDtypeStruct((2, 192, 256), BF)...]
where the time goes in v4:
time: 57.3 us; the launch traced here: 57.2 us
  Pallas kernels  56.4 us (98%)
  between operations  0.8 us (1%)
    pallas_call x1, Pallas kernels, body(): pl.pallas_call(kernel, out_shape=(jax.ShapeDtypeStruct((2, 192, 256), BF)...  54.9 us
    pallas_call x1, Pallas kernels, body(): pl.pallas_call(widen, out_shape=(jax.ShapeDtypeStruct((192, 256), BF), ja...  1.53 us

profile of v4, /device:TPU:1, one launch (start us, length us, event | category | flops | bytes accessed | tf_op | source)
XLA Modules:
  0.0 57.2 jit_solution(2139025746226936290)
XLA Ops:
  0.6 54.9 %shard_map.85 = (bf16[2,192,256]{2,1,0:T(8,128)(2,1)S(1)}, bf16[2,3,4,192,128]{4,3,2,1,0:T(8,128)(2,1)S(1)}) custom-call(bf16[4080,1536]{1,0:T(8,128)(2,1)} %bitcast.13, bf16[1536,256]{1,0:T(8,128)(2,1)} %bitcast.16, bf16[3072,256]{1,0:T(8,128)(2,1)} %bitcast.14, bf16[192,256]{1,0:T(8,128)(2,1)} %bitcast.17, bf16[192,256]{1,0:T(8,128)(2,1)} %bitcast.18, ...), custom_call_target="tpu_custom_call" | custom-call | tf_op jit(solution)/shard_map/pallas_call | solution.py:570
  55.5 1.5 %shard_map.86 = (bf16[192,256]{1,0:T(8,128)(2,1)}, bf16[192,256]{1,0:T(8,128)(2,1)}, f32[2304,256]{1,0:T(8,128)}) custom-call(bf16[2,192,256]{2,1,0:T(8,128)(2,1)S(1)} %get-tuple-element.8.og, bf16[2,2304,128]{2,1,0:T(8,128)(2,1)S(1)} %bitcast.12), custom_call_target="tpu_custom_call" | custom-call | tf_op jit(solution)/shard_map/pallas_call | solution.py:614

commit v5 on v4

--- a/solution.py
+++ b/solution.py
@@ -50,7 +50,7 @@
     g_hbm, q_hbm, k_hbm, qi_hbm, ki_hbm, cw_hbm,
     og_out, w_out,
     g, qv, kv, cw, pool, pool_t, mid, fine, kt, qt,
-    c0r, s1, r1, s2, r2, s3, r3, d0s, d0r,
+    c0r, s1, r1, s2, r2, s3, r3, d0s, d0r, e1s, e1r, e2s, e2r,
     eye, perm, mean1, mean2, mean3, up3, up2, up1,
     stage, colp, rowp, padt, win_t, wacc,
     a0r, a1s, a1r, a2, a3, a4, ogs,
@@ -177,6 +177,8 @@
         return cs * pitch + rs if s % 2 else rs * pitch + cs
 
     flight = {}
+    slot = {0: 0, 1: 1, 2: 2, 4: 3, 5: 4}
+    place = {3: 0, 6: 1}
 
     @jax.named_scope("tables")
     def tables():
@@ -291,8 +293,8 @@
             beyond = (3 - first) if c == 0 else flip
             for j in range(4):
                 n = first if j < 2 else beyond
-                s1[u, c, j] = part_of(u, j % 2, n, c).astype(BF)
-            flight[u, 1] = send(s1.at[u, c], r1.at[u, c], ring(u, first), 3, sem, r1.at[u])
+                s1[slot[u], c, j] = part_of(u, j % 2, n, c).astype(BF)
+            flight[u, 1] = send(s1.at[slot[u], c], r1.at[slot[u], c], ring(u, first), 3, sem, r1.at[slot[u]])
 
     @jax.named_scope("step2")
     def step2(u):
@@ -301,8 +303,8 @@
         for c in range(2):
             _, second = mates(u)[c]
             for j in range(2):
-                s2[u, c, j] = (part_of(u, j, second, c) + r1[u, c, 2 + j].astype(F32)).astype(BF)
-            flight[u, 2] = send(s2.at[u, c], r2.at[u, c], ring(u, second), 4, sem, r2.at[u])
+                s2[slot[u], c, j] = (part_of(u, j, second, c) + r1[slot[u], c, 2 + j].astype(F32)).astype(BF)
+            flight[u, 2] = send(s2.at[slot[u], c], r2.at[slot[u], c], ring(u, second), 4, sem, r2.at[slot[u]])
 
     @jax.named_scope("step3")
     def step3(u):
@@ -310,9 +312,9 @@
         _, n, z = along(u)
         arrived(flight[u, 2])
         for c in range(2):
-            far = part_of(u, 1 - z, n, c) + r1[u, c, 1 - z].astype(F32) + r2[u, c, 1 - z].astype(F32)
-            s3[u, c] = far.astype(BF)
-            flight[u, 3] = send(s3.at[u, c], r3.at[u, c], last_mate(u), 5, sem, r3.at[u])
+            far = part_of(u, 1 - z, n, c) + r1[slot[u], c, 1 - z].astype(F32) + r2[slot[u], c, 1 - z].astype(F32)
+            s3[slot[u], c] = far.astype(BF)
+            flight[u, 3] = send(s3.at[slot[u], c], r3.at[slot[u], c], last_mate(u), 5, sem, r3.at[slot[u]])
 
     @jax.named_scope("finish")
     def finish(u):
@@ -321,9 +323,47 @@
         at = 48 * (u % 4)
         arrived(flight[u, 3])
         for c in range(2):
-            total = part_of(u, z, n, c) + r1[u, c, z].astype(F32) + r2[u, c, z].astype(F32)
-            total = (total + r3[u, c].astype(F32)) * 0.0625
+            total = part_of(u, z, n, c) + r1[slot[u], c, z].astype(F32) + r2[slot[u], c, z].astype(F32)
+            total = (total + r3[slot[u], c].astype(F32)) * 0.0625
             stage[s, at:at + 48, 128 * c:128 * c + 128] = total.astype(BF)
+
+    def whole_part(u, z, n):
+        return kt[u, core, z * 4 + n] if u < 4 else qt[u - 4, z * 4 + n]
+
+    @jax.named_scope("scatter")
+    def scatter(u):
+        dim, n, _ = along(u)
+        e = place[u]
+        sem = group()
+        for k in range(4):
+            for z in range(2):
+                e1s[e, k, z] = whole_part(u, z, k).astype(BF)
+        for d in (1, 2, 3):
+            flight[u, 1] = send(
+                e1s.at[e, (n + d) % 4], e1r.at[e, d - 1], shift(dim, d), 13, sem, e1r.at[e]
+            )
+
+    @jax.named_scope("pair")
+    def pair(u):
+        _, n, z = along(u)
+        e = place[u]
+        arrived(flight[u, 1])
+        far = whole_part(u, 1 - z, n)
+        for k in range(3):
+            far = far + e1r[e, k, 1 - z].astype(F32)
+        e2s[e] = far.astype(BF)
+        flight[u, 2] = send(e2s.at[e], e2r.at[e], last_mate(u), 14, group(), e2r.at[e])
+
+    @jax.named_scope("pair_finish")
+    def pair_finish(u):
+        _, n, z = along(u)
+        e = place[u]
+        total = whole_part(u, z, n)
+        for k in range(3):
+            total = total + e1r[e, k, z].astype(F32)
+        arrived(flight[u, 2])
+        at = 48 * (u % 4)
+        stage[3 if u < 4 else 2, at:at + 48, :] = ((total + e2r[e].astype(F32)) * 0.0625).astype(BF)
 
     @jax.named_scope("direct")
     def direct():
@@ -350,7 +390,10 @@
     def core_step(u):
         arrived(flight[u, 0])
         kt[u, core] = kt[u, core] + c0r[u]
-        step1(u)
+        if u == 3:
+            scatter(u)
+        else:
+            step1(u)
 
     @jax.named_scope("image_windows")
     def image_windows(s):
@@ -419,52 +462,52 @@
         key_tiles(i)
         core_send(i)
 
+    def queries(i):
+        query_chunk(i)
+        step1(4 + i)
+
     keys(1)
     core_step(0)
     keys(2)
     core_step(1)
     ld_g[3].wait()
-
-    def queries(i):
-        query_chunk(i)
-        step1(4 + i)
-
+    keys(3)
+    core_step(2)
     queries(0)
-    core_step(2)
+    core_step(3)
     step2(0)
-    keys(3)
     hr = []
     for s in range(2):
         arrived(hc[s])
         hr.append(halo_rows(s))
     queries(1)
     step2(1)
-    core_step(3)
-    queries(2)
-    step3(0)
+    query_chunk(2)
     step2(2)
     step2(4)
+    scatter(6)
     query_chunk(3)
+    step2(5)
     direct()
-    step2(5)
-    step2(3)
+    pair(3)
+    step3(0)
     step3(1)
     arrived(hr[1])
     image_windows(1)
-    step2(6)
     step3(2)
     step3(4)
     arrived(hr[0])
     image_windows(0)
-    step3(3)
+    pair(6)
     step3(5)
-    step3(6)
-    for u in range(4):
+    for u in range(3):
         finish(u)
+    pair_finish(3)
     hk = halo_cols(3)
     weight_part(1, True)
-    for u in range(4, 7):
+    for u in range(4, 6):
         finish(u)
+    pair_finish(6)
     direct_finish()
     hq = halo_cols(2)
     weight_part(0, False)
@@ -536,7 +579,7 @@
         f6.append(send(mine, mine, other_core, 11, group(), mine))
     for j in range(3):
         arrived(f6[j])
-    sent = (colp, rowp, c0r, s1, s2, s3, a0r, a1r, a1r, a1r, a1r, a1s, d0r)
+    sent = (colp, rowp, c0r, s1, s2, s3, a0r, a1r, a1r, a1r, a1r, a1s, d0r, e1r, e2r)
     for k, ref in enumerate(sent):
         pltpu.make_async_copy(ref, ref, send_sem.at[k]).wait()
     copies[0].wait()
@@ -580,10 +623,11 @@
             vmem(4096, 256), vmem(256, 4096), vmem(768, 256), vmem(2, 768, 256, dtype=F32),
             vmem(4, 2, 8, 48, 256, dtype=F32), vmem(4, 8, 48, 256, dtype=F32),
             vmem(4, 8, 48, 256, dtype=F32),
-            vmem(7, 2, 4, 48, 128), vmem(7, 2, 4, 48, 128),
-            vmem(7, 2, 2, 48, 128), vmem(7, 2, 2, 48, 128),
-            vmem(7, 2, 48, 128), vmem(7, 2, 48, 128),
+            vmem(5, 2, 4, 48, 128), vmem(5, 2, 4, 48, 128),
+            vmem(5, 2, 2, 48, 128), vmem(5, 2, 2, 48, 128),
+            vmem(5, 2, 48, 128), vmem(5, 2, 48, 128),
             vmem(8, 48, 256), vmem(7, 48, 256),
+            vmem(2, 4, 2, 48, 256), vmem(2, 3, 2, 48, 256), vmem(2, 48, 256), vmem(2, 48, 256),
             vmem(256, 256), vmem(256, 256), vmem(128, 512), vmem(64, 1024), vmem(48, 3072),
             vmem(192, 48), vmem(768, 192), vmem(768, 192),
             vmem(4, ST, 256), vmem(4, 32, 256), vmem(4, 64, 256),
@@ -592,8 +636,8 @@
             vmem(3, 4, 192, 128), vmem(3, 3, 192, 128),
             vmem(3, 4, 192, 128), vmem(3, 4, 192, 128), vmem(3, 192, 128), vmem(2, 192, 256),
             pltpu.SemaphoreType.DMA((16,)),
-            pltpu.SemaphoreType.DMA((13,)),
-            pltpu.SemaphoreType.DMA((52,)),
+            pltpu.SemaphoreType.DMA((15,)),
+            pltpu.SemaphoreType.DMA((50,)),
         ],
         compiler_params=pltpu.CompilerParams(
             collective_id=0, has_side_effects=True, vmem_limit_bytes=VMEM_BYTES

time: 57.3 us -> 56.7 us (0.990)
  Pallas kernels: 56.4 us -> 55.8 us
where the time goes in v5:
time: 56.7 us; the launch traced here: 56.6 us
  Pallas kernels  55.8 us (98%)
  between operations  0.8 us (1%)
    pallas_call x1, Pallas kernels, body(): pl.pallas_call(kernel, out_shape=(jax.ShapeDtypeStruct((2, 192, 256), BF)...  54.3 us
    pallas_call x1, Pallas kernels, body(): pl.pallas_call(widen, out_shape=(jax.ShapeDtypeStruct((192, 256), BF), ja...  1.53 us

profile of v5, /device:TPU:1, one launch (start us, length us, event | category | flops | bytes accessed | tf_op | source)
XLA Modules:
  0.0 56.6 jit_solution(2702305075159869651)
XLA Ops:
  0.6 54.3 %shard_map.85 = (bf16[2,192,256]{2,1,0:T(8,128)(2,1)S(1)}, bf16[2,3,4,192,128]{4,3,2,1,0:T(8,128)(2,1)S(1)}) custom-call(bf16[4080,1536]{1,0:T(8,128)(2,1)} %bitcast.13, bf16[1536,256]{1,0:T(8,128)(2,1)} %bitcast.16, bf16[3072,256]{1,0:T(8,128)(2,1)} %bitcast.14, bf16[192,256]{1,0:T(8,128)(2,1)} %bitcast.17, bf16[192,256]{1,0:T(8,128)(2,1)} %bitcast.18, ...), custom_call_target="tpu_custom_call" | custom-call | tf_op jit(solution)/shard_map/pallas_call | solution.py:613
  54.9 1.5 %shard_map.86 = (bf16[192,256]{1,0:T(8,128)(2,1)}, bf16[192,256]{1,0:T(8,128)(2,1)}, f32[2304,256]{1,0:T(8,128)}) custom-call(bf16[2,192,256]{2,1,0:T(8,128)(2,1)S(1)} %get-tuple-element.8.og, bf16[2,2304,128]{2,1,0:T(8,128)(2,1)S(1)} %bitcast.12), custom_call_target="tpu_custom_call" | custom-call | tf_op jit(solution)/shard_map/pallas_call | solution.py:658

commit v6 on v5

--- a/solution.py
+++ b/solution.py
@@ -53,7 +53,7 @@
     c0r, s1, r1, s2, r2, s3, r3, d0s, d0r, e1s, e1r, e2s, e2r,
     eye, perm, mean1, mean2, mean3, up3, up2, up1,
     stage, colp, rowp, padt, win_t, wacc,
-    a0r, a1s, a1r, a2, a3, a4, ogs,
+    a0s, a0r, a1s, a1r, a2, a3, a4, ogs,
     in_sem, send_sem, recv_sem,
 ):
     pb, ka = lax.axis_index("pb"), lax.axis_index("ka")
@@ -420,7 +420,8 @@
                 rows = slice(256 * k, 256 * k + 256)
                 wacc[h, j, rows] = half if first else wacc[h, j, rows] + half
             if not first and k == 2:
-                f0.append(send(wacc.at[1 - core, j], a0r.at[j], other_core, 6, group(), a0r.at[j]))
+                a0s[j] = wacc[1 - core, j].astype(BF)
+                f0.append(send(a0s.at[j], a0r.at[j], other_core, 6, group(), a0r.at[j]))
 
     @jax.named_scope("input_grad")
     def input_grad(s, slot):
@@ -517,7 +518,7 @@
     for j in range(3):
         arrived(f0[j])
         n = coords[j]
-        wacc[core, j] = wacc[core, j] + a0r[j]
+        wacc[core, j] = wacc[core, j] + a0r[j].astype(F32)
         for k in range(4):
             a1s[j, k] = wacc[core, j, 192 * k:192 * k + 192].astype(BF)
         sem = group()
@@ -632,7 +633,7 @@
             vmem(192, 48), vmem(768, 192), vmem(768, 192),
             vmem(4, ST, 256), vmem(4, 32, 256), vmem(4, 64, 256),
             vmem(2, 256, QP), vmem(2, 9, 256, 192), vmem(2, 3, 768, 128, dtype=F32),
-            vmem(3, 768, 128, dtype=F32),
+            vmem(3, 768, 128), vmem(3, 768, 128),
             vmem(3, 4, 192, 128), vmem(3, 3, 192, 128),
             vmem(3, 4, 192, 128), vmem(3, 4, 192, 128), vmem(3, 192, 128), vmem(2, 192, 256),
             pltpu.SemaphoreType.DMA((16,)),

time: 56.7 us -> 56.6 us (level)
  no operation moved by 1% of the time
where the time goes in v6:
time: 56.6 us; the launch traced here: 56.5 us
  Pallas kernels  55.7 us (98%)
  between operations  0.8 us (1%)
    pallas_call x1, Pallas kernels, body(): pl.pallas_call(kernel, out_shape=(jax.ShapeDtypeStruct((2, 192, 256), BF)...  54.2 us
    pallas_call x1, Pallas kernels, body(): pl.pallas_call(widen, out_shape=(jax.ShapeDtypeStruct((192, 256), BF), ja...  1.53 us

profile of v6, /device:TPU:1, one launch (start us, length us, event | category | flops | bytes accessed | tf_op | source)
XLA Modules:
  0.0 56.5 jit_solution(343403108707958254)
XLA Ops:
  0.6 54.2 %shard_map.85 = (bf16[2,192,256]{2,1,0:T(8,128)(2,1)S(1)}, bf16[2,3,4,192,128]{4,3,2,1,0:T(8,128)(2,1)S(1)}) custom-call(bf16[4080,1536]{1,0:T(8,128)(2,1)} %bitcast.13, bf16[1536,256]{1,0:T(8,128)(2,1)} %bitcast.16, bf16[3072,256]{1,0:T(8,128)(2,1)} %bitcast.14, bf16[192,256]{1,0:T(8,128)(2,1)} %bitcast.17, bf16[192,256]{1,0:T(8,128)(2,1)} %bitcast.18, ...), custom_call_target="tpu_custom_call" | custom-call | tf_op jit(solution)/shard_map/pallas_call | solution.py:614
  54.8 1.5 %shard_map.86 = (bf16[192,256]{1,0:T(8,128)(2,1)}, bf16[192,256]{1,0:T(8,128)(2,1)}, f32[2304,256]{1,0:T(8,128)}) custom-call(bf16[2,192,256]{2,1,0:T(8,128)(2,1)S(1)} %get-tuple-element.8.og, bf16[2,2304,128]{2,1,0:T(8,128)(2,1)S(1)} %bitcast.12), custom_call_target="tpu_custom_call" | custom-call | tf_op jit(solution)/shard_map/pallas_call | solution.py:659
